TPU v7x, 128 devices: a whole 4x4x4 slice. The times are simulated.
128 devices in a mesh: expert: 8 (over x, core), hidden: 16 (over z, y).
Axes of the slice: x: 4, y: 4, z: 4, core: 2. Of those that a mesh axis runs over, the one named last changes fastest.
Arguments:
- hidden_in: bfloat16 [2048, 6144], P(('expert', 'hidden')), may hold values from -6 to 6
- norm_gain: float32 [6144], replicated, may hold values from 0.25 to 1.75
- router_weight: bfloat16 [6144, 8], replicated, may hold values from -0.078125 to 0.078125
- expert_ids: int32 [2048, 2], P(('expert', 'hidden')), may hold values from 0 to 7, all different within a row; in each aligned block of 16 rows (0 to 15, 16 to 31, ...) at most 6 rows name the same one
- gate_proj: bfloat16 [8, 6144, 8192], P('expert', None, 'hidden'), may hold values from -0.078125 to 0.078125
- up_proj: bfloat16 [8, 6144, 8192], P('expert', None, 'hidden'), may hold values from -0.078125 to 0.078125
- down_proj: bfloat16 [8, 8192, 6144], P('expert', 'hidden'), may hold values from -0.0625 to 0.0625
Outputs:
- layer_out: bfloat16 [2048, 6144], P(('expert', 'hidden'))
Inputs may be any that keep to these rules, and one draw needn't show every extreme that they name: `expert_ids`: the two experts of a token differ. Within the rows of one device (aligned blocks of 16 tokens) no expert is named by more than 6 rows, a bound that some block reaches.
All inputs are finite; a program needn't handle non-finite values.
Results may differ from a plain program's by a relative error of at most 0.0085.
Values may be sent and summed in bfloat16 or wider, within the bound.
No kernel may reach another device: no remote copies, remote signals or barrier semaphores. Data moves between devices by JAX's collectives and lax.ppermute only.
A program may use at most 128 MiB of HBM per device.

v0:
```python
import jax
import jax.numpy as jnp
from jax import lax
from jax.sharding import PartitionSpec as P


def normalize(hidden_in, norm_gain):
    values = hidden_in.astype(jnp.float32)
    factor = lax.rsqrt(jnp.mean(values * values, axis=-1, keepdims=True) + 1e-05)
    return (values * factor * norm_gain).astype(jnp.bfloat16)


def gate_weights(normed, router_weight, expert_ids, experts):
    logits = jnp.dot(normed, router_weight, preferred_element_type=jnp.float32)
    picks = expert_ids[:, :, None] == jnp.arange(experts, dtype=jnp.int32)[None, None, :]
    chosen = jnp.sum(jnp.where(picks, logits[:, None, :], 0.0), axis=-1)
    first = jax.nn.sigmoid(chosen[:, 0] - chosen[:, 1])
    return jnp.stack([first, 1.0 - first], axis=1)


def route_slots(block_ids, experts, capacity):
    flat_ids = block_ids.reshape(-1)
    onehot = (flat_ids[:, None] == jnp.arange(experts, dtype=jnp.int32)[None, :]).astype(jnp.int32)
    before = jnp.cumsum(onehot, axis=0) - onehot
    rank_in = jnp.sum(before * onehot, axis=1)
    slot_place = flat_ids * capacity + rank_in
    owners = jnp.arange(flat_ids.shape[0], dtype=jnp.int32) // block_ids.shape[1]
    slot_token = jnp.zeros((experts * capacity,), jnp.int32).at[slot_place].set(owners)
    filled = jnp.zeros((experts * capacity,), jnp.bfloat16).at[slot_place].set(1.0)
    return (slot_place, slot_token, filled)


def per_device(hidden_in, norm_gain, router_weight, expert_ids, gate_proj, up_proj, down_proj):
    experts = lax.axis_size("expert")
    hidden_count = lax.axis_size("hidden")
    tok_rows = hidden_in.shape[0]
    width = hidden_in.shape[1]
    top_count = expert_ids.shape[1]
    capacity = 3 * tok_rows * top_count // (2 * experts)
    normed = normalize(hidden_in, norm_gain)
    gates = gate_weights(normed, router_weight, expert_ids, experts)
    slot_place, slot_token, filled = route_slots(expert_ids, experts, capacity)
    outgoing = (jnp.take(normed, slot_token, axis=0) * filled[:, None]).reshape(
        experts, capacity, width
    )
    gate_local = gate_proj[0]
    up_local = up_proj[0]
    down_local = down_proj[0]
    copies = jnp.broadcast_to(outgoing[:, None], (experts, hidden_count, capacity, width))
    copies = copies.reshape(experts * hidden_count, capacity, width)
    arrived = lax.all_to_all(copies, ("expert", "hidden"), split_axis=0, concat_axis=0, tiled=True)
    piece = arrived.reshape(experts * hidden_count * capacity, width)
    gate = jnp.dot(piece, gate_local, preferred_element_type=jnp.float32)
    upper = jnp.dot(piece, up_local, preferred_element_type=jnp.float32)
    inner = (jax.nn.silu(gate) * upper).astype(jnp.bfloat16)
    inner = inner.reshape(experts, hidden_count, capacity, inner.shape[1]).transpose(1, 0, 2, 3)
    inner = inner.reshape(hidden_count * experts * capacity, inner.shape[3])
    piece = inner
    own_rows = lax.psum_scatter(
        jnp.dot(piece, down_local, preferred_element_type=jnp.float32).astype(jnp.bfloat16),
        "hidden",
        scatter_dimension=0,
        tiled=True,
    )
    answers = own_rows.reshape(experts, capacity, width)
    returned = lax.all_to_all(answers, "expert", split_axis=0, concat_axis=0, tiled=True).reshape(
        experts * capacity, width
    )
    picked = (
        jnp.take(returned, slot_place, axis=0)
        .reshape(tok_rows, top_count, width)
        .astype(jnp.float32)
    )
    mixture = jnp.sum(gates[:, :, None] * picked, axis=1)
    return (hidden_in.astype(jnp.float32) + mixture).astype(jnp.bfloat16)


def solution(mesh):
    placed = (
        P(("expert", "hidden"), None),
        P(),
        P(),
        P(("expert", "hidden"), None),
        P("expert", None, "hidden"),
        P("expert", None, "hidden"),
        P("expert", "hidden", None),
    )
    return jax.shard_map(
        per_device,
        mesh=mesh,
        in_specs=placed,
        out_specs=P(("expert", "hidden"), None),
        check_vma=False,
    )
```

profile of v0, /device:TPU:1, one launch (start us, length us, event | category | flops | bytes accessed | tf_op | source)
XLA Modules:
  0.0 334.7 jit_solution(17215063068767753839)
XLA Ops:
  6.5 0.7 broadcast_multiply_fusion
  7.3 0.8 copy.28
  8.6 0.7 scatter_custom_fusion
  9.3 1.1 fusion.11
  10.5 0.8 scatter_custom_fusion.1
  11.4 1.0 fusion.13
  12.4 0.9 gather_fusion
  13.7 6.0 %broadcast_in_dim.70 = bf16[8,16,6,6144]{3,2,1,0:T(8,128)(2,1)} broadcast(bf16[8,6,6144]{2,1,0:T(8,128)(2,1)S(1)} %select_multiply_fusion), dimensions={0,2,3} | broadcast | bytes 10027008 | tf_op jit(solution)/shard_map/broadcast_in_dim | solution.py:49
  19.8 153.8 %all_to_all.10 = bf16[128,6,6144]{2,1,0:T(8,128)(2,1)} all-to-all(bf16[128,6,6144]{2,1,0:T(8,128)(2,1)} %bitcast.28), channel_id=1, replica_groups=mesh['expert'=8,'hidden'=16] {'expert','hidden'}, dimensions={0} | all-to-all | bytes 18874368 | tf_op jit(solution)/shard_map/all_to_all | solution.py:51
  173.6 14.3 %reshape.104 = bf16[768,6144]{1,0:T(8,128)(2,1)} reshape(bf16[128,6,6144]{2,1,0:T(8,128)(2,1)} %all_to_all.10) | data formatting | bytes 18874368 | tf_op jit(solution)/shard_map/reshape | solution.py:52
  187.8 9.6 %fusion.3 = f32[768,512]{1,0:T(8,128)S(1)} fusion(bf16[768,6144]{1,0:T(8,128)(2,1)} %reshape.104, bf16[1,6144,512]{2,1,0:T(8,128)(2,1)} %param.11), kind=kOutput, calls=%fused_computation.8 | convolution fusion | flops 4831838208 | bytes 17301504 | tf_op jit(solution)/shard_map/dot_general | solution.py:53
  197.4 7.2 %fusion.8 = bf16[768,512]{1,0:T(8,128)(2,1)S(1)} fusion(bf16[768,6144]{1,0:T(8,128)(2,1)S(1)} %copy-done.1, bf16[1,6144,512]{2,1,0:T(8,128)(2,1)} %param.12, f32[768,512]{1,0:T(8,128)S(1)} %fusion.3), kind=kOutput, calls=%fused_computation.11 | convolution fusion | flops 4834197504 | bytes 18087936 | tf_op jit(solution)/shard_map/dot_general | solution.py:54
  204.6 0.3 reshape.105
  205.0 0.3 reshape.106
  205.3 10.2 %convolution_convert_fusion = bf16[768,6144]{1,0:T(8,128)(2,1)} fusion(bf16[768,512]{1,0:T(8,128)(2,1)S(1)} %reshape.106, bf16[1,512,6144]{2,1,0:T(8,128)(2,1)} %param.13), kind=kOutput, calls=%fused_computation.4 | convolution fusion | flops 4836556800 | bytes 16515072 | tf_op jit(solution)/shard_map/dot_general | solution.py:60
  215.7 0.5 copy-done.3
  216.4 87.5 %reduce-scatter.2.cloned.1.call-done = bf16[48,6144]{1,0:T(8,128)(2,1)} async-done(((bf16[768,6144]{1,0:T(8,128)(2,1)}), bf16[48,6144]{1,0:T(8,128)(2,1)}) %reduce-scatter.2.cloned.1.call-update) | async-done | bytes 589840 | tf_op jit(solution)/shard_map/reduce_scatter | solution.py:59
  303.9 2.1 reshape.107
  306.1 6.3 %all-to-all-start.1 = ((bf16[8,6,6144]{2,1,0:T(8,128)(2,1)}), bf16[8,6,6144]{2,1,0:T(8,128)(2,1)S(1)}, u32[]{:S(2)}, u32[]{:S(2)}) async-start(bf16[8,6,6144]{2,1,0:T(8,128)(2,1)} %reshape.107), calls=%async_computation.2 | async-start | bytes 1572864 | tf_op jit(solution)/shard_map/all_to_all | solution.py:66
  312.5 12.0 %all-to-all-done.1 = bf16[8,6,6144]{2,1,0:T(8,128)(2,1)S(1)} async-done(((bf16[8,6,6144]{2,1,0:T(8,128)(2,1)}), bf16[8,6,6144]{2,1,0:T(8,128)(2,1)S(1)}, u32[]{:S(2)}, u32[]{:S(2)}) %all-to-all-start.1) | async-done | bytes 589856 | tf_op jit(solution)/shard_map/all_to_all | solution.py:66
  324.8 0.8 gather_fusion.1
  325.6 0.3 gather.15
  325.8 1.2 multiply_reduce_fusion
  327.1 0.7 fusion.14
  (38 shorter events, 2.1 us)
Async XLA Ops:
  6.5 209.7 %copy-start = (bf16[6144,8]{0,1:T(8,128)(2,1)S(1)}, bf16[6144,8]{0,1:T(8,128)(2,1)}, u32[]{:S(2)}) copy-start(bf16[6144,8]{0,1:T(8,128)(2,1)} %param.9) | copy-start | bytes 294916
  6.5 297.4 %reduce-scatter.2.cloned.1.call-start = ((), (), s32[]{:S(2)}) async-start(), calls=%async_computation.3 | async-start | bytes 10027008 | tf_op jit(solution)/shard_map/reduce_scatter | solution.py:59
  187.8 9.6 %copy-start.1 = (bf16[768,6144]{1,0:T(8,128)(2,1)S(1)}, bf16[768,6144]{1,0:T(8,128)(2,1)}, u32[]{:S(2)}) copy-start(bf16[768,6144]{1,0:T(8,128)(2,1)} %reshape.104) | copy-start | bytes 28311556
  215.5 0.7 copy-start.3
  215.5 111.6 %copy-start.2 = (bf16[16,6144]{1,0:T(8,128)(2,1)S(1)}, bf16[16,6144]{1,0:T(8,128)(2,1)}, u32[]{:S(2)}) copy-start(bf16[16,6144]{1,0:T(8,128)(2,1)} %param.7) | copy-start | bytes 589828
  306.1 18.5 %all-to-all-start.1 = ((bf16[8,6,6144]{2,1,0:T(8,128)(2,1)}), bf16[8,6,6144]{2,1,0:T(8,128)(2,1)S(1)}, u32[]{:S(2)}, u32[]{:S(2)}) async-start(bf16[8,6,6144]{2,1,0:T(8,128)(2,1)} %reshape.107), calls=%async_computation.2 | async-start | bytes 1572864 | tf_op jit(solution)/shard_map/all_to_all | solution.py:66
Sparse Core Ops, SparseCore 0:
  215.6 88.2 reduce-scatter.1
where the time goes:
time: 335 us
  blocking collectives  154 us (46%)
  waiting for transfers between devices  99.5 us (30%)
  local copies, waits for them, and re-layouts  28.9 us (9%)
  matrix products  27.2 us (8%)
  between operations  13.6 us (4%)
  starting transfers between devices  6.32 us (2%)
  other arithmetic  5.37 us (2%)
    all_to_all x1, blocking collectives, per_device(): lax.all_to_all(copies, ('expert', 'hidden'), split_axis=0, concat_axis=0,...  154 us
    reduce_scatter x1, waiting for transfers between devices, per_device(): lax.psum_scatter(jnp.dot(piece, down_local, preferred_element_type=jnp.fl...  87.5 us
    reshape x1, local copies, waits for them, and re-layouts, per_device(): piece = arrived.reshape(experts * hidden_count * capacity, width)  14.3 us
    all_to_all x1, waiting for transfers between devices, per_device(): lax.all_to_all(answers, 'expert', split_axis=0, concat_axis=0, tiled=True)  12 us
    dot_general x1, matrix products, per_device(): jnp.dot(piece, down_local, preferred_element_type=jnp.float32)  10.2 us
    dot_general x1, matrix products, per_device(): gate = jnp.dot(piece, gate_local, preferred_element_type=jnp.float32)  9.56 us
    dot_general x1, matrix products, per_device(): upper = jnp.dot(piece, up_local, preferred_element_type=jnp.float32)  7.22 us
  transfers between devices with their start and end apart: 2, of which 2 were waited for; matrix products, arithmetic and copies ran while one was open for 0% of the time, Pallas kernels for 0%

commit v1 on v0

v1 whole, which is shorter than its diff:
```python
import jax
import jax.numpy as jnp
from jax import lax
from jax.experimental import pallas as pl
from jax.experimental.pallas import tpu as pltpu
from jax.sharding import PartitionSpec as P


RING = 4


PAD = 8
CHUNK = 512


def slots(ids_ref):
    first, second = ids_ref[0:1, :], ids_ref[1:2, :]
    tokens = first.shape[1]
    down = lax.broadcasted_iota(jnp.int32, (tokens, tokens), 0)
    across = lax.broadcasted_iota(jnp.int32, (tokens, tokens), 1)

    def column(row):
        return jnp.sum(jnp.where(down == across, row, 0), axis=1, keepdims=True)

    first_col, second_col = column(first), column(second)
    found = []
    for ids in (first, second):
        same = (first_col == ids).astype(jnp.int32) + (second_col == ids).astype(jnp.int32)
        rank = jnp.sum(jnp.where(down < across, same, 0), axis=0, keepdims=True)
        found.append((ids, rank))
    same = (first == second).astype(jnp.int32)
    return [found[0][0] * PAD + found[0][1], found[1][0] * PAD + found[1][1] + same]


def route_kernel(hidden_ref, gain_ref, ids_ref, out_ref, normed_ref):
    experts, capacity, width = out_ref.shape
    tokens = hidden_ref.shape[0]
    values = hidden_ref[...].astype(jnp.float32)
    factor = lax.rsqrt(jnp.sum(values * values, axis=1, keepdims=True) / width + 1e-05)
    normed_ref[...] = (values * factor * gain_ref[...]).astype(jnp.bfloat16)
    first, second = slots(ids_ref)
    place = lax.broadcasted_iota(jnp.int32, (experts * PAD, tokens), 0)
    pick = jnp.where((place == first) | (place == second), 1.0, 0.0).astype(jnp.bfloat16)

    @pl.loop(0, width // CHUNK)
    def _(step):
        columns = pl.ds(pl.multiple_of(step * CHUNK, CHUNK), CHUNK)
        rows = jnp.dot(pick, normed_ref[:, columns], preferred_element_type=jnp.float32)
        for e in range(experts):
            out_ref[e, :, columns] = rows[e * PAD : e * PAD + capacity].astype(jnp.bfloat16)


def gate_kernel(normed_ref, router_ref, ids_ref, out_ref):
    logits = lax.dot_general(
        router_ref[...], normed_ref[...], (((1,), (1,)), ((), ())), preferred_element_type=jnp.float32
    )
    expert = lax.broadcasted_iota(jnp.int32, logits.shape, 0)
    chosen = [
        jnp.sum(jnp.where(expert == ids_ref[k : k + 1, :], logits, 0.0), axis=0, keepdims=True)
        for k in range(2)
    ]
    gate = 1.0 / (1.0 + jnp.exp(chosen[1] - chosen[0]))
    first, second = slots(ids_ref)
    place = lax.broadcasted_iota(jnp.int32, out_ref.shape, 0)
    out_ref[...] = jnp.where(place == first, gate, 0.0) + jnp.where(place == second, 1.0 - gate, 0.0)


def mix_kernel(hidden_ref, weight_ref, rows_ref, out_ref, held_ref):
    experts, capacity, width = rows_ref.shape
    held_ref[...] = jnp.zeros_like(held_ref)
    weight = weight_ref[...]

    @pl.loop(0, width // CHUNK)
    def _(step):
        columns = pl.ds(pl.multiple_of(step * CHUNK, CHUNK), CHUNK)
        for e in range(experts):
            held_ref[e * PAD : e * PAD + capacity, :] = rows_ref[e, :, columns].astype(jnp.float32)
        mixed = lax.dot_general(
            weight,
            held_ref[...],
            (((0,), (0,)), ((), ())),
            precision=lax.Precision.HIGHEST,
            preferred_element_type=jnp.float32,
        )
        out_ref[:, columns] = (hidden_ref[:, columns].astype(jnp.float32) + mixed).astype(jnp.bfloat16)


def shift(value, axis, step):
    def target(i):
        z, y = divmod(i, RING)
        return ((z + step) % RING) * RING + y if axis == "z" else z * RING + (y + step) % RING

    return lax.ppermute(value, "hidden", [(i, target(i)) for i in range(RING * RING)])


def gather_ring(own, first, second):
    half = own.shape[1] // 2
    below, above = shift(own, first, 1), shift(own, first, -1)
    across = [shift(below[:, :half], first, 1), shift(above[:, half:], first, -1)]
    mine = jnp.concatenate([own, below, above, jnp.concatenate(across, axis=1)], axis=0)
    mine = lax.optimization_barrier(mine)
    rows = mine.shape[0] // 2
    below, above = shift(mine, second, 1), shift(mine, second, -1)
    far = [shift(below[:rows], second, 1), shift(above[rows:], second, -1)]
    return [mine], [below, above], far


def add(*terms):
    total = terms[0].astype(jnp.float32)
    for term in terms[1:]:
        total = total + term.astype(jnp.float32)
    return total.astype(jnp.bfloat16)


def low_add(value, low, half):
    return jnp.concatenate([add(value[:, :half], low), value[:, half:]], axis=1)


def high_add(value, high, half):
    return jnp.concatenate([value[:, :half], add(value[:, half:], high)], axis=1)


def reduce_ring(inner, down, first, second, rows):
    half = down.shape[1] // 2

    def product(blocks, weight):
        value = jnp.concatenate(blocks, axis=0)
        value = jnp.dot(value, weight, preferred_element_type=jnp.float32)
        return lax.optimization_barrier(value.astype(jnp.bfloat16))

    low, high = down[:, :half], down[:, half:]
    early = [inner[b][3] for b in range(3)]
    late = [inner[3][3]]
    lows = [shift(product(t, low), first, 1) for t in (early, late)]
    highs = [shift(product(t, high), first, -1) for t in (early, late)]
    above = product([inner[b][2] for b in range(4)], down)
    below = product([inner[b][1] for b in range(4)], down)
    own = product([inner[b][0] for b in range(4)], down)
    above = shift(low_add(above, jnp.concatenate(lows, axis=0), half), first, 1)
    below = shift(high_add(below, jnp.concatenate(highs, axis=0), half), first, -1)
    own = add(own, above, below)
    across = own[3 * rows :]
    low = shift(across[:, :half], second, 1)
    high = shift(across[:, half:], second, -1)
    above = shift(low_add(own[2 * rows : 3 * rows], low, half), second, 1)
    below = shift(high_add(own[rows : 2 * rows], high, half), second, -1)
    return add(own[:rows], above, below)


def per_device(hidden_in, norm_gain, router_weight, expert_ids, gate_proj, up_proj, down_proj):
    experts = lax.axis_size("expert")
    tok_rows = hidden_in.shape[0]
    width = hidden_in.shape[1]
    top_count = expert_ids.shape[1]
    capacity = 3 * tok_rows * top_count // (2 * experts)
    rows = experts * capacity
    ids = expert_ids.T
    outgoing, normed = pl.pallas_call(
        route_kernel,
        out_shape=(
            jax.ShapeDtypeStruct((experts, capacity, width), jnp.bfloat16),
            jax.ShapeDtypeStruct((tok_rows, width), jnp.bfloat16),
        ),
        name="route",
    )(hidden_in, norm_gain.reshape(1, width), ids)
    weights = pl.pallas_call(
        gate_kernel,
        out_shape=jax.ShapeDtypeStruct((experts * PAD, tok_rows), jnp.float32),
        name="gates",
    )(normed, router_weight.T, ids)
    gate_local = gate_proj[0]
    up_local = up_proj[0]
    down_local = down_proj[0]
    arrived = lax.all_to_all(outgoing, "expert", split_axis=0, concat_axis=0, tiled=True)
    arrived = arrived.reshape(rows, width)
    part = rows // 2
    orders = (("z", "y"), ("y", "z"))
    gathered = [gather_ring(arrived[i * part : (i + 1) * part], *orders[i]) for i in range(2)]
    inner = [[], []]
    for stage in range(3):
        value = jnp.concatenate(gathered[0][stage] + gathered[1][stage], axis=0)
        gate = jnp.dot(value, gate_local, preferred_element_type=jnp.float32)
        upper = jnp.dot(value, up_local, preferred_element_type=jnp.float32)
        act = (jax.nn.silu(gate) * upper).astype(jnp.bfloat16)
        act = act.reshape(2, -1, RING, part, act.shape[1])
        for i in range(2):
            inner[i] += [[act[i, b, a] for a in range(RING)] for b in range(act.shape[1])]
    answers = [reduce_ring(inner[i], down_local, *orders[i], part) for i in range(2)]
    answers = jnp.concatenate(answers, axis=0).reshape(experts, capacity, width)
    returned = lax.all_to_all(answers, "expert", split_axis=0, concat_axis=0, tiled=True)
    return pl.pallas_call(
        mix_kernel,
        out_shape=jax.ShapeDtypeStruct((tok_rows, width), jnp.bfloat16),
        scratch_shapes=[pltpu.VMEM((experts * PAD, CHUNK), jnp.float32)],
        name="mix",
    )(hidden_in, weights, returned)


def solution(mesh):
    placed = (
        P(("expert", "hidden"), None),
        P(),
        P(),
        P(("expert", "hidden"), None),
        P("expert", None, "hidden"),
        P("expert", None, "hidden"),
        P("expert", "hidden", None),
    )

    return jax.shard_map(
        per_device,
        mesh=mesh,
        in_specs=placed,
        out_specs=P(("expert", "hidden"), None),
        check_vma=False,
    )
```

time: 335 us -> 194 us (0.58)
  blocking collectives: 154 us -> 17.9 us
  starting transfers between devices: 6.32 us -> 70.4 us
  waiting for transfers between devices: 99.5 us -> 63.1 us
  local copies, waits for them, and re-layouts: 28.9 us -> 3.34 us
  between operations: 13.6 us -> 0.72 us
  Pallas kernels: 0 us -> 10.3 us
    all_to_all x1, blocking collectives: 154 us -> 17.9 us  [per_device(): lax.all_to_all(outgoing, 'expert', split_axis=0, concat_axis=0, tiled=True)]
    reduce_scatter x1 -> x0, waiting for transfers between devices: 87.5 us -> none  [per_device(): lax.psum_scatter(jnp.dot(piece, down_local, preferred_element_type=jnp.fl...]
    ppermute x0 -> x36, starting transfers between devices: none -> 52.9 us  [shift(): lax.ppermute(value, 'hidden', [(i, target(i)) for i in range(RING * RING)])]
    ppermute x0 -> x36, waiting for transfers between devices: none -> 52.8 us  [shift(): lax.ppermute(value, 'hidden', [(i, target(i)) for i in range(RING * RING)])]
    reshape x6 -> x1, local copies, waits for them, and re-layouts: 17.2 us -> 1.12 us  [per_device(): answers = jnp.concatenate(answers, axis=0).reshape(experts, capacity, width)]
    all_to_all x1, starting transfers between devices: 6.32 us -> 17.6 us  [per_device(): lax.all_to_all(answers, 'expert', split_axis=0, concat_axis=0, tiled=True)]
    pallas_call x0 -> x3, Pallas kernels: none -> 10.3 us  [the longest x1 4.86 us: per_device(): pl.pallas_call(mix_kernel, out_shape=jax.ShapeDtypeStruct((tok_rows, widt...]
    broadcast_in_dim x3 -> x0, local copies, waits for them, and re-layouts: 6.13 us -> none  [the longest x1 6.04 us: per_device(): jnp.broadcast_to(outgoing[:, None], (experts, hidden_count, capacity, wid...]
  transfers between devices with their start and end apart: 2 -> 37, of which waited for: 2 -> 12; matrix products, arithmetic and copies ran while one was open for 0% -> 11% of each run, Pallas kernels for 0% -> 1%
where the time goes in v1:
time: 194 us
  starting transfers between devices  70.4 us (36%)
  waiting for transfers between devices  63.1 us (33%)
  matrix products  25.5 us (13%)
  blocking collectives  17.9 us (9%)
  Pallas kernels  10.3 us (5%)
  local copies, waits for them, and re-layouts  3.34 us (2%)
  other arithmetic  2.45 us (1%)
    ppermute x36, starting transfers between devices, shift(): lax.ppermute(value, 'hidden', [(i, target(i)) for i in range(RING * RING)])  52.9 us
    ppermute x36, waiting for transfers between devices, shift(): lax.ppermute(value, 'hidden', [(i, target(i)) for i in range(RING * RING)])  52.8 us
    all_to_all x1, blocking collectives, per_device(): lax.all_to_all(outgoing, 'expert', split_axis=0, concat_axis=0, tiled=True)  17.9 us
    all_to_all x1, starting transfers between devices, per_device(): lax.all_to_all(answers, 'expert', split_axis=0, concat_axis=0, tiled=True)  17.6 us
    dot_general x14, matrix products, product(): value = jnp.dot(value, weight, preferred_element_type=jnp.float32)  11.8 us
    all_to_all x1, waiting for transfers between devices, per_device(): lax.all_to_all(answers, 'expert', split_axis=0, concat_axis=0, tiled=True)  10.4 us
    dot_general x3, matrix products, per_device(): gate = jnp.dot(value, gate_local, preferred_element_type=jnp.float32)  8.33 us
    dot_general x3, matrix products, per_device(): upper = jnp.dot(value, up_local, preferred_element_type=jnp.float32)  5.42 us
  transfers between devices with their start and end apart: 37, of which 12 were waited for; matrix products, arithmetic and copies ran while one was open for 11% of the time, Pallas kernels for 1%

profile of v1, /device:TPU:1, one launch (start us, length us, event | category | flops | bytes accessed | tf_op | source)
XLA Modules:
  0.0 193.8 jit_solution(6123938061509106010)
XLA Ops:
  0.0 3.7 %route.1 = (bf16[8,6,6144]{2,1,0:T(8,128)(2,1)}, bf16[16,6144]{1,0:T(8,128)(2,1)}) custom-call(bf16[16,6144]{1,0:T(8,128)(2,1)} %hidden_ref.3, f32[1,6144]{1,0:T(1,128)} %bitcast.147, s32[2,16]{1,0:T(2,128)} %bitcast.148), custom_call_target="tpu_custom_call" | custom-call | tf_op jit(solution)/shard_map/route/pallas_call | solution.py:158
  3.7 17.9 %all_to_all.10 = bf16[8,6,6144]{2,1,0:T(8,128)(2,1)S(1)} all-to-all(bf16[8,6,6144]{2,1,0:T(8,128)(2,1)} %get-tuple-element.8), channel_id=1, replica_groups=mesh['expert'=8,'hidden'=16] {'expert'}, dimensions={0} | all-to-all | bytes 1179648 | tf_op jit(solution)/shard_map/all_to_all | solution.py:174
  21.8 2.8 %collective-permute-start.5 = (bf16[24,6144]{1,0:T(8,128)(2,1)S(1)}, bf16[24,6144]{1,0:T(8,128)(2,1)S(1)}, u32[]{:S(2)}, u32[]{:S(2)}) collective-permute-start(bf16[24,6144]{1,0:T(8,128)(2,1)S(1)} %slice.229), channel_id=1, source_target_pairs={{0,3},{1,0},{2,1},{3,2},{4,7},{5,4},{6,5},{7,6},{8,11},{9,8},{10,9... | collective-permute-start | bytes 884744 | tf_op jit(solution)/shard_map/ppermute | solution.py:93
  24.7 3.8 %collective-permute-start.1 = (bf16[24,6144]{1,0:T(8,128)(2,1)S(1)}, bf16[24,6144]{1,0:T(8,128)(2,1)S(1)}, u32[]{:S(2)}, u32[]{:S(2)}) collective-permute-start(bf16[24,6144]{1,0:T(8,128)(2,1)S(1)} %slice.225), channel_id=1, source_target_pairs={{0,12},{1,13},{2,14},{3,15},{4,0},{5,1},{6,2},{7,3},{8,4},{9,5},{1... | collective-permute-start | bytes 884744 | tf_op jit(solution)/shard_map/ppermute | solution.py:93
  29.9 3.5 %collective-permute-start.7 = (bf16[24,3072]{1,0:T(8,128)(2,1)S(1)}, bf16[24,3072]{1,0:T(8,128)(2,1)S(1)}, u32[]{:S(2)}, u32[]{:S(2)}) collective-permute-start(bf16[24,3072]{1,0:T(8,128)(2,1)S(1)} %slice.297), channel_id=1, source_target_pairs={{0,3},{1,0},{2,1},{3,2},{4,7},{5,4},{6,5},{7,6},{8,11},{9,8},{10,9... | collective-permute-start | bytes 442376 | tf_op jit(solution)/shard_map/ppermute | solution.py:93
  33.6 3.8 %collective-permute-start.3 = (bf16[24,3072]{1,0:T(8,128)(2,1)S(1)}, bf16[24,3072]{1,0:T(8,128)(2,1)S(1)}, u32[]{:S(2)}, u32[]{:S(2)}) collective-permute-start(bf16[24,3072]{1,0:T(8,128)(2,1)S(1)} %slice.294), channel_id=1, source_target_pairs={{0,12},{1,13},{2,14},{3,15},{4,0},{5,1},{6,2},{7,3},{8,4},{9,5},{1... | collective-permute-start | bytes 442376 | tf_op jit(solution)/shard_map/ppermute | solution.py:93
  38.8 3.8 %collective-permute-start.11 = (bf16[96,6144]{1,0:T(8,128)(2,1)S(1)}, bf16[96,6144]{1,0:T(8,128)(2,1)S(1)}, u32[]{:S(2)}, u32[]{:S(2)}) collective-permute-start(bf16[96,6144]{1,0:T(8,128)(2,1)S(1)} %maximum_maximum_fusion.1), channel_id=1, source_target_pairs={{0,12},{1,13},{2,14},{3,15},{4,0},{5,1},{6,2},{7,3},{8,4},{9,5},{1... | collective-permute-start | bytes 3538952 | tf_op jit(solution)/shard_map/ppermute | solution.py:93
  42.7 2.7 %collective-permute-start.9 = (bf16[96,6144]{1,0:T(8,128)(2,1)S(1)}, bf16[96,6144]{1,0:T(8,128)(2,1)S(1)}, u32[]{:S(2)}, u32[]{:S(2)}) collective-permute-start(bf16[96,6144]{1,0:T(8,128)(2,1)S(1)} %maximum_maximum_fusion), channel_id=1, source_target_pairs={{0,3},{1,0},{2,1},{3,2},{4,7},{5,4},{6,5},{7,6},{8,11},{9,8},{10,9... | collective-permute-start | bytes 3538952 | tf_op jit(solution)/shard_map/ppermute | solution.py:93
  45.5 4.4 %fusion.10 = f32[192,512]{1,0:T(8,128)S(1)} fusion(bf16[1,6144,512]{2,1,0:T(8,128)(2,1)} %param.11, bf16[96,6144]{1,0:T(8,128)(2,1)S(1)} %maximum_maximum_fusion.1, bf16[96,6144]{1,0:T(8,128)(2,1)S(1)} %maximum_maximum_fusion), kind=kOutput, calls=%fused_computation.16 | convolution fusion | flops 1212678144 | bytes 9043968 | tf_op jit(solution)/shard_map/dot_general | solution.py:182
  51.3 17.1 %collective-permute-done.8 = bf16[96,6144]{1,0:T(8,128)(2,1)S(1)} collective-permute-done((bf16[96,6144]{1,0:T(8,128)(2,1)S(1)}, bf16[96,6144]{1,0:T(8,128)(2,1)S(1)}, u32[]{:S(2)}, u32[]{:S(2)}) %collective-permute-start.8) | collective-permute-done | bytes 1179680 | tf_op jit(solution)/shard_map/ppermute | solution.py:93
  77.3 3.0 %collective-permute-start.13 = (bf16[48,6144]{1,0:T(8,128)(2,1)S(1)}, bf16[48,6144]{1,0:T(8,128)(2,1)S(1)}, u32[]{:S(2)}, u32[]{:S(2)}) collective-permute-start(bf16[48,6144]{1,0:T(8,128)(2,1)S(1)} %slice.302), channel_id=1, source_target_pairs={{0,3},{1,0},{2,1},{3,2},{4,7},{5,4},{6,5},{7,6},{8,11},{9,8},{10,9... | collective-permute-start | bytes 1769480 | tf_op jit(solution)/shard_map/ppermute | solution.py:93
  81.9 10.1 %collective-permute-done.12 = bf16[48,6144]{1,0:T(8,128)(2,1)S(1)} collective-permute-done((bf16[48,6144]{1,0:T(8,128)(2,1)S(1)}, bf16[48,6144]{1,0:T(8,128)(2,1)S(1)}, u32[]{:S(2)}, u32[]{:S(2)}) %collective-permute-start.12) | collective-permute-done | bytes 589856 | tf_op jit(solution)/shard_map/ppermute | solution.py:93
  93.4 2.9 %collective-permute-start.29 = (bf16[72,3072]{1,0:T(8,128)(2,1)S(1)}, bf16[72,3072]{1,0:T(8,128)(2,1)S(1)}, u32[]{:S(2)}, u32[]{:S(2)}) collective-permute-start(bf16[72,3072]{1,0:T(8,128)(2,1)S(1)} %convolution_convert_fusion.6), channel_id=1, source_target_pairs={{0,3},{1,0},{2,1},{3,2},{4,7},{5,4},{6,5},{7,6},{8,11},{9,8},{10,9... | collective-permute-start | bytes 1327112 | tf_op jit(solution)/shard_map/ppermute | solution.py:93
  114.5 3.0 %collective-permute-start.21 = (bf16[96,6144]{1,0:T(8,128)(2,1)S(1)}, bf16[96,6144]{1,0:T(8,128)(2,1)S(1)}, u32[]{:S(2)}, u32[]{:S(2)}) collective-permute-start(bf16[96,6144]{1,0:T(8,128)(2,1)S(1)} %pad_maximum_fusion.6), channel_id=1, source_target_pairs={{0,12},{1,13},{2,14},{3,15},{4,0},{5,1},{6,2},{7,3},{8,4},{9,5},{1... | collective-permute-start | bytes 3538952 | tf_op jit(solution)/shard_map/ppermute | solution.py:93
  118.1 2.7 %collective-permute-start.31 = (bf16[96,6144]{1,0:T(8,128)(2,1)S(1)}, bf16[96,6144]{1,0:T(8,128)(2,1)S(1)}, u32[]{:S(2)}, u32[]{:S(2)}) collective-permute-start(bf16[96,6144]{1,0:T(8,128)(2,1)S(1)} %pad_maximum_fusion.8), channel_id=1, source_target_pairs={{0,3},{1,0},{2,1},{3,2},{4,7},{5,4},{6,5},{7,6},{8,11},{9,8},{10,9... | collective-permute-start | bytes 3538952 | tf_op jit(solution)/shard_map/ppermute | solution.py:93
  120.9 12.4 %collective-permute-done.18 = bf16[96,6144]{1,0:T(8,128)(2,1)S(1)} collective-permute-done((bf16[96,6144]{1,0:T(8,128)(2,1)S(1)}, bf16[96,6144]{1,0:T(8,128)(2,1)S(1)}, u32[]{:S(2)}, u32[]{:S(2)}) %collective-permute-start.18) | collective-permute-done | bytes 1179680 | tf_op jit(solution)/shard_map/ppermute | solution.py:93
  133.2 3.0 %collective-permute-done.21 = bf16[96,6144]{1,0:T(8,128)(2,1)S(1)} collective-permute-done((bf16[96,6144]{1,0:T(8,128)(2,1)S(1)}, bf16[96,6144]{1,0:T(8,128)(2,1)S(1)}, u32[]{:S(2)}, u32[]{:S(2)}) %collective-permute-start.21) | collective-permute-done | bytes 1179680 | tf_op jit(solution)/shard_map/ppermute | solution.py:93
  140.0 3.2 %collective-permute-start.34 = (bf16[24,3072]{1,0:T(8,128)(2,1)S(1)}, bf16[24,3072]{1,0:T(8,128)(2,1)S(1)}, u32[]{:S(2)}, u32[]{:S(2)}) collective-permute-start(bf16[24,3072]{1,0:T(8,128)(2,1)S(1)} %get-tuple-element.18), channel_id=1, source_target_pairs={{0,12},{1,13},{2,14},{3,15},{4,0},{5,1},{6,2},{7,3},{8,4},{9,5},{1... | collective-permute-start | bytes 442376 | tf_op jit(solution)/shard_map/ppermute | solution.py:93
  144.0 2.7 %collective-permute-start.25 = (bf16[24,6144]{1,0:T(8,128)(2,1)S(1)}, bf16[24,6144]{1,0:T(8,128)(2,1)S(1)}, u32[]{:S(2)}, u32[]{:S(2)}) collective-permute-start(bf16[24,6144]{1,0:T(8,128)(2,1)S(1)} %pad_maximum_fusion.13), channel_id=1, source_target_pairs={{0,3},{1,0},{2,1},{3,2},{4,7},{5,4},{6,5},{7,6},{8,11},{9,8},{10,9... | collective-permute-start | bytes 884744 | tf_op jit(solution)/shard_map/ppermute | solution.py:93
  146.9 3.2 %collective-permute-start.35 = (bf16[24,6144]{1,0:T(8,128)(2,1)S(1)}, bf16[24,6144]{1,0:T(8,128)(2,1)S(1)}, u32[]{:S(2)}, u32[]{:S(2)}) collective-permute-start(bf16[24,6144]{1,0:T(8,128)(2,1)S(1)} %pad_maximum_fusion.15), channel_id=1, source_target_pairs={{0,12},{1,13},{2,14},{3,15},{4,0},{5,1},{6,2},{7,3},{8,4},{9,5},{1... | collective-permute-start | bytes 884744 | tf_op jit(solution)/shard_map/ppermute | solution.py:93
  150.3 3.3 %collective-permute-done.25 = bf16[24,6144]{1,0:T(8,128)(2,1)S(1)} collective-permute-done((bf16[24,6144]{1,0:T(8,128)(2,1)S(1)}, bf16[24,6144]{1,0:T(8,128)(2,1)S(1)}, u32[]{:S(2)}, u32[]{:S(2)}) %collective-permute-start.25) | collective-permute-done | bytes 294944 | tf_op jit(solution)/shard_map/ppermute | solution.py:93
  158.3 17.6 %all-to-all-start.1 = ((bf16[8,6,6144]{2,1,0:T(8,128)(2,1)}), bf16[8,6,6144]{2,1,0:T(8,128)(2,1)S(1)}, u32[]{:S(2)}, u32[]{:S(2)}) async-start(bf16[8,6,6144]{2,1,0:T(8,128)(2,1)} %reshape.22), calls=%async_computation.1 | async-start | bytes 1572864 | tf_op jit(solution)/shard_map/all_to_all | solution.py:190
  177.7 10.4 %all-to-all-done.1.rows_ref = bf16[8,6,6144]{2,1,0:T(8,128)(2,1)S(1)} async-done(((bf16[8,6,6144]{2,1,0:T(8,128)(2,1)}), bf16[8,6,6144]{2,1,0:T(8,128)(2,1)S(1)}, u32[]{:S(2)}, u32[]{:S(2)}) %all-to-all-start.1) | async-done | bytes 589856 | tf_op jit(solution)/shard_map/all_to_all | solution.py:190
  189.0 4.9 %mix.1 = bf16[16,6144]{1,0:T(8,128)(2,1)} custom-call(bf16[16,6144]{1,0:T(8,128)(2,1)} %hidden_ref.3, f32[64,16]{1,0:T(8,128)} %gates.1.weight_ref, bf16[8,6,6144]{2,1,0:T(8,128)(2,1)} %copy-done), custom_call_target="tpu_custom_call" | custom-call | tf_op jit(solution)/shard_map/mix/pallas_call | solution.py:191
  (142 shorter events, 47.3 us)
Async XLA Ops:
  24.6 8.8 %collective-permute-start.4 = (bf16[24,6144]{1,0:T(8,128)(2,1)S(1)}, bf16[24,6144]{1,0:T(8,128)(2,1)S(1)}, u32[]{:S(2)}, u32[]{:S(2)}) collective-permute-start(bf16[24,6144]{1,0:T(8,128)(2,1)S(1)} %slice.229), channel_id=1, source_target_pairs={{0,1},{1,2},{2,3},{3,0},{4,5},{5,6},{6,7},{7,4},{8,9},{9,10},{10,1... | collective-permute-start | bytes 884744 | tf_op jit(solution)/shard_map/ppermute | solution.py:93
  24.7 8.9 %collective-permute-start.1 = (bf16[24,6144]{1,0:T(8,128)(2,1)S(1)}, bf16[24,6144]{1,0:T(8,128)(2,1)S(1)}, u32[]{:S(2)}, u32[]{:S(2)}) collective-permute-start(bf16[24,6144]{1,0:T(8,128)(2,1)S(1)} %slice.225), channel_id=1, source_target_pairs={{0,12},{1,13},{2,14},{3,15},{4,0},{5,1},{6,2},{7,3},{8,4},{9,5},{1... | collective-permute-start | bytes 884744 | tf_op jit(solution)/shard_map/ppermute | solution.py:93
  28.5 8.8 %collective-permute-start = (bf16[24,6144]{1,0:T(8,128)(2,1)S(1)}, bf16[24,6144]{1,0:T(8,128)(2,1)S(1)}, u32[]{:S(2)}, u32[]{:S(2)}) collective-permute-start(bf16[24,6144]{1,0:T(8,128)(2,1)S(1)} %slice.225), channel_id=1, source_target_pairs={{0,4},{1,5},{2,6},{3,7},{4,8},{5,9},{6,10},{7,11},{8,12},{9,13},{1... | collective-permute-start | bytes 884744 | tf_op jit(solution)/shard_map/ppermute | solution.py:93
  33.6 9.0 %collective-permute-start.3 = (bf16[24,3072]{1,0:T(8,128)(2,1)S(1)}, bf16[24,3072]{1,0:T(8,128)(2,1)S(1)}, u32[]{:S(2)}, u32[]{:S(2)}) collective-permute-start(bf16[24,3072]{1,0:T(8,128)(2,1)S(1)} %slice.294), channel_id=1, source_target_pairs={{0,12},{1,13},{2,14},{3,15},{4,0},{5,1},{6,2},{7,3},{8,4},{9,5},{1... | collective-permute-start | bytes 442376 | tf_op jit(solution)/shard_map/ppermute | solution.py:93
  38.8 29.9 %collective-permute-start.11 = (bf16[96,6144]{1,0:T(8,128)(2,1)S(1)}, bf16[96,6144]{1,0:T(8,128)(2,1)S(1)}, u32[]{:S(2)}, u32[]{:S(2)}) collective-permute-start(bf16[96,6144]{1,0:T(8,128)(2,1)S(1)} %maximum_maximum_fusion.1), channel_id=1, source_target_pairs={{0,12},{1,13},{2,14},{3,15},{4,0},{5,1},{6,2},{7,3},{8,4},{9,5},{1... | collective-permute-start | bytes 3538952 | tf_op jit(solution)/shard_map/ppermute | solution.py:93
  42.6 26.0 %collective-permute-start.10 = (bf16[96,6144]{1,0:T(8,128)(2,1)S(1)}, bf16[96,6144]{1,0:T(8,128)(2,1)S(1)}, u32[]{:S(2)}, u32[]{:S(2)}) collective-permute-start(bf16[96,6144]{1,0:T(8,128)(2,1)S(1)} %maximum_maximum_fusion.1), channel_id=1, source_target_pairs={{0,4},{1,5},{2,6},{3,7},{4,8},{5,9},{6,10},{7,11},{8,12},{9,13},{1... | collective-permute-start | bytes 3538952 | tf_op jit(solution)/shard_map/ppermute | solution.py:93
  42.7 25.8 %collective-permute-start.9 = (bf16[96,6144]{1,0:T(8,128)(2,1)S(1)}, bf16[96,6144]{1,0:T(8,128)(2,1)S(1)}, u32[]{:S(2)}, u32[]{:S(2)}) collective-permute-start(bf16[96,6144]{1,0:T(8,128)(2,1)S(1)} %maximum_maximum_fusion), channel_id=1, source_target_pairs={{0,3},{1,0},{2,1},{3,2},{4,7},{5,4},{6,5},{7,6},{8,11},{9,8},{10,9... | collective-permute-start | bytes 3538952 | tf_op jit(solution)/shard_map/ppermute | solution.py:93
  45.4 23.0 %collective-permute-start.8 = (bf16[96,6144]{1,0:T(8,128)(2,1)S(1)}, bf16[96,6144]{1,0:T(8,128)(2,1)S(1)}, u32[]{:S(2)}, u32[]{:S(2)}) collective-permute-start(bf16[96,6144]{1,0:T(8,128)(2,1)S(1)} %maximum_maximum_fusion), channel_id=1, source_target_pairs={{0,1},{1,2},{2,3},{3,0},{4,5},{5,6},{6,7},{7,4},{8,9},{9,10},{10,1... | collective-permute-start | bytes 3538952 | tf_op jit(solution)/shard_map/ppermute | solution.py:93
  75.6 20.7 %collective-permute-start.15 = (bf16[48,6144]{1,0:T(8,128)(2,1)S(1)}, bf16[48,6144]{1,0:T(8,128)(2,1)S(1)}, u32[]{:S(2)}, u32[]{:S(2)}) collective-permute-start(bf16[48,6144]{1,0:T(8,128)(2,1)S(1)} %slice.304), channel_id=1, source_target_pairs={{0,12},{1,13},{2,14},{3,15},{4,0},{5,1},{6,2},{7,3},{8,4},{9,5},{1... | collective-permute-start | bytes 1769480 | tf_op jit(solution)/shard_map/ppermute | solution.py:93
  76.8 16.6 %collective-permute-start.14 = (bf16[48,6144]{1,0:T(8,128)(2,1)S(1)}, bf16[48,6144]{1,0:T(8,128)(2,1)S(1)}, u32[]{:S(2)}, u32[]{:S(2)}) collective-permute-start(bf16[48,6144]{1,0:T(8,128)(2,1)S(1)} %slice.303), channel_id=1, source_target_pairs={{0,4},{1,5},{2,6},{3,7},{4,8},{5,9},{6,10},{7,11},{8,12},{9,13},{1... | collective-permute-start | bytes 1769480 | tf_op jit(solution)/shard_map/ppermute | solution.py:93
  77.3 15.9 %collective-permute-start.13 = (bf16[48,6144]{1,0:T(8,128)(2,1)S(1)}, bf16[48,6144]{1,0:T(8,128)(2,1)S(1)}, u32[]{:S(2)}, u32[]{:S(2)}) collective-permute-start(bf16[48,6144]{1,0:T(8,128)(2,1)S(1)} %slice.302), channel_id=1, source_target_pairs={{0,3},{1,0},{2,1},{3,2},{4,7},{5,4},{6,5},{7,6},{8,11},{9,8},{10,9... | collective-permute-start | bytes 1769480 | tf_op jit(solution)/shard_map/ppermute | solution.py:93
  80.3 11.7 %collective-permute-start.12 = (bf16[48,6144]{1,0:T(8,128)(2,1)S(1)}, bf16[48,6144]{1,0:T(8,128)(2,1)S(1)}, u32[]{:S(2)}, u32[]{:S(2)}) collective-permute-start(bf16[48,6144]{1,0:T(8,128)(2,1)S(1)} %slice.301), channel_id=1, source_target_pairs={{0,1},{1,2},{2,3},{3,0},{4,5},{5,6},{6,7},{7,4},{8,9},{9,10},{10,1... | collective-permute-start | bytes 1769480 | tf_op jit(solution)/shard_map/ppermute | solution.py:93
  81.8 27.0 %collective-permute-start.16 = (bf16[72,3072]{1,0:T(8,128)(2,1)S(1)}, bf16[72,3072]{1,0:T(8,128)(2,1)S(1)}, u32[]{:S(2)}, u32[]{:S(2)}) collective-permute-start(bf16[72,3072]{1,0:T(8,128)(2,1)S(1)} %convolution_convert_fusion.9), channel_id=1, source_target_pairs={{0,4},{1,5},{2,6},{3,7},{4,8},{5,9},{6,10},{7,11},{8,12},{9,13},{1... | collective-permute-start | bytes 1327112 | tf_op jit(solution)/shard_map/ppermute | solution.py:93
  92.0 19.6 %collective-permute-start.19 = (bf16[72,3072]{1,0:T(8,128)(2,1)S(1)}, bf16[72,3072]{1,0:T(8,128)(2,1)S(1)}, u32[]{:S(2)}, u32[]{:S(2)}) collective-permute-start(bf16[72,3072]{1,0:T(8,128)(2,1)S(1)} %convolution_convert_fusion.8), channel_id=1, source_target_pairs={{0,12},{1,13},{2,14},{3,15},{4,0},{5,1},{6,2},{7,3},{8,4},{9,5},{1... | collective-permute-start | bytes 1327112 | tf_op jit(solution)/shard_map/ppermute | solution.py:93
  93.2 21.3 %collective-permute-start.26 = (bf16[72,3072]{1,0:T(8,128)(2,1)S(1)}, bf16[72,3072]{1,0:T(8,128)(2,1)S(1)}, u32[]{:S(2)}, u32[]{:S(2)}) collective-permute-start(bf16[72,3072]{1,0:T(8,128)(2,1)S(1)} %convolution_convert_fusion.7), channel_id=1, source_target_pairs={{0,1},{1,2},{2,3},{3,0},{4,5},{5,6},{6,7},{7,4},{8,9},{9,10},{10,1... | collective-permute-start | bytes 1327112 | tf_op jit(solution)/shard_map/ppermute | solution.py:93
  93.4 24.5 %collective-permute-start.29 = (bf16[72,3072]{1,0:T(8,128)(2,1)S(1)}, bf16[72,3072]{1,0:T(8,128)(2,1)S(1)}, u32[]{:S(2)}, u32[]{:S(2)}) collective-permute-start(bf16[72,3072]{1,0:T(8,128)(2,1)S(1)} %convolution_convert_fusion.6), channel_id=1, source_target_pairs={{0,3},{1,0},{2,1},{3,2},{4,7},{5,4},{6,5},{7,6},{8,11},{9,8},{10,9... | collective-permute-start | bytes 1327112 | tf_op jit(solution)/shard_map/ppermute | solution.py:93
  100.3 8.6 %collective-permute-start.17 = (bf16[24,3072]{1,0:T(8,128)(2,1)S(1)}, bf16[24,3072]{1,0:T(8,128)(2,1)S(1)}, u32[]{:S(2)}, u32[]{:S(2)}) collective-permute-start(bf16[24,3072]{1,0:T(8,128)(2,1)S(1)} %convolution_convert_fusion.13), channel_id=1, source_target_pairs={{0,4},{1,5},{2,6},{3,7},{4,8},{5,9},{6,10},{7,11},{8,12},{9,13},{1... | collective-permute-start | bytes 442376 | tf_op jit(solution)/shard_map/ppermute | solution.py:93
  108.8 8.7 %collective-permute-start.27 = (bf16[24,3072]{1,0:T(8,128)(2,1)S(1)}, bf16[24,3072]{1,0:T(8,128)(2,1)S(1)}, u32[]{:S(2)}, u32[]{:S(2)}) collective-permute-start(bf16[24,3072]{1,0:T(8,128)(2,1)S(1)} %convolution_convert_fusion.11), channel_id=1, source_target_pairs={{0,1},{1,2},{2,3},{3,0},{4,5},{5,6},{6,7},{7,4},{8,9},{9,10},{10,1... | collective-permute-start | bytes 442376 | tf_op jit(solution)/shard_map/ppermute | solution.py:93
  114.3 19.0 %collective-permute-start.18 = (bf16[96,6144]{1,0:T(8,128)(2,1)S(1)}, bf16[96,6144]{1,0:T(8,128)(2,1)S(1)}, u32[]{:S(2)}, u32[]{:S(2)}) collective-permute-start(bf16[96,6144]{1,0:T(8,128)(2,1)S(1)} %pad_maximum_fusion.5), channel_id=1, source_target_pairs={{0,4},{1,5},{2,6},{3,7},{4,8},{5,9},{6,10},{7,11},{8,12},{9,13},{1... | collective-permute-start | bytes 3538952 | tf_op jit(solution)/shard_map/ppermute | solution.py:93
  114.5 21.7 %collective-permute-start.21 = (bf16[96,6144]{1,0:T(8,128)(2,1)S(1)}, bf16[96,6144]{1,0:T(8,128)(2,1)S(1)}, u32[]{:S(2)}, u32[]{:S(2)}) collective-permute-start(bf16[96,6144]{1,0:T(8,128)(2,1)S(1)} %pad_maximum_fusion.6), channel_id=1, source_target_pairs={{0,12},{1,13},{2,14},{3,15},{4,0},{5,1},{6,2},{7,3},{8,4},{9,5},{1... | collective-permute-start | bytes 3538952 | tf_op jit(solution)/shard_map/ppermute | solution.py:93
  117.8 21.7 %collective-permute-start.28 = (bf16[96,6144]{1,0:T(8,128)(2,1)S(1)}, bf16[96,6144]{1,0:T(8,128)(2,1)S(1)}, u32[]{:S(2)}, u32[]{:S(2)}) collective-permute-start(bf16[96,6144]{1,0:T(8,128)(2,1)S(1)} %pad_maximum_fusion.7), channel_id=1, source_target_pairs={{0,1},{1,2},{2,3},{3,0},{4,5},{5,6},{6,7},{7,4},{8,9},{9,10},{10,1... | collective-permute-start | bytes 3538952 | tf_op jit(solution)/shard_map/ppermute | solution.py:93
  118.1 21.3 %collective-permute-start.31 = (bf16[96,6144]{1,0:T(8,128)(2,1)S(1)}, bf16[96,6144]{1,0:T(8,128)(2,1)S(1)}, u32[]{:S(2)}, u32[]{:S(2)}) collective-permute-start(bf16[96,6144]{1,0:T(8,128)(2,1)S(1)} %pad_maximum_fusion.8), channel_id=1, source_target_pairs={{0,3},{1,0},{2,1},{3,2},{4,7},{5,4},{6,5},{7,6},{8,11},{9,8},{10,9... | collective-permute-start | bytes 3538952 | tf_op jit(solution)/shard_map/ppermute | solution.py:93
  144.0 9.6 %collective-permute-start.25 = (bf16[24,6144]{1,0:T(8,128)(2,1)S(1)}, bf16[24,6144]{1,0:T(8,128)(2,1)S(1)}, u32[]{:S(2)}, u32[]{:S(2)}) collective-permute-start(bf16[24,6144]{1,0:T(8,128)(2,1)S(1)} %pad_maximum_fusion.13), channel_id=1, source_target_pairs={{0,3},{1,0},{2,1},{3,2},{4,7},{5,4},{6,5},{7,6},{8,11},{9,8},{10,9... | collective-permute-start | bytes 884744 | tf_op jit(solution)/shard_map/ppermute | solution.py:93
  158.3 29.7 %all-to-all-start.1 = ((bf16[8,6,6144]{2,1,0:T(8,128)(2,1)}), bf16[8,6,6144]{2,1,0:T(8,128)(2,1)S(1)}, u32[]{:S(2)}, u32[]{:S(2)}) async-start(bf16[8,6,6144]{2,1,0:T(8,128)(2,1)} %reshape.22), calls=%async_computation.1 | async-start | bytes 1572864 | tf_op jit(solution)/shard_map/all_to_all | solution.py:190
  (20 other events, 157.7 us)

commit v2 on v1

v2 whole, which is shorter than its diff:
```python
import functools

import jax
import jax.numpy as jnp
from jax import lax
from jax.experimental import pallas as pl
from jax.experimental.pallas import tpu as pltpu
from jax.sharding import PartitionSpec as P


RING = 4


PAD = 8
CHUNK = 512
MIX = 1024
TILE = 16


def slots(ids_ref):
    first, second = ids_ref[0:1, :], ids_ref[1:2, :]
    tokens = first.shape[1]
    down = lax.broadcasted_iota(jnp.int32, (tokens, tokens), 0)
    across = lax.broadcasted_iota(jnp.int32, (tokens, tokens), 1)

    def column(row):
        return jnp.sum(jnp.where(down == across, row, 0), axis=1, keepdims=True)

    first_col, second_col = column(first), column(second)
    here = lax.axis_index("expert")
    found = []
    for ids, extra in ((first, 0), (second, (first == second).astype(jnp.int32))):
        same = (first_col == ids).astype(jnp.int32) + (second_col == ids).astype(jnp.int32)
        rank = jnp.sum(jnp.where(down < across, same, 0), axis=0, keepdims=True) + extra
        offset = ((ids >> 1) - (here >> 1)) & (RING - 1)
        place = jnp.where(offset == 0, 0, jnp.where(offset == RING - 1, 1, offset + 1))
        found.append((place, (ids & 1) ^ (here & 1), rank))
    return found


def route_kernel(hidden_ref, gain_ref, ids_ref, same_ref, other_ref, normed_ref):
    count, capacity, width = same_ref.shape
    tokens = hidden_ref.shape[0]
    values = hidden_ref[...].astype(jnp.float32)
    factor = lax.rsqrt(jnp.sum(values * values, axis=1, keepdims=True) / width + 1e-05)
    normed_ref[...] = (values * factor * gain_ref[...]).astype(jnp.bfloat16)
    first, second = [(core * count + place) * PAD + rank for place, core, rank in slots(ids_ref)]
    row = lax.broadcasted_iota(jnp.int32, (2 * count * PAD, tokens), 0)
    pick = jnp.where((row == first) | (row == second), 1.0, 0.0).astype(jnp.bfloat16)

    @pl.loop(0, width // CHUNK)
    def _(step):
        columns = pl.ds(pl.multiple_of(step * CHUNK, CHUNK), CHUNK)
        rows = jnp.dot(pick, normed_ref[:, columns], preferred_element_type=jnp.float32)
        for i in range(count):
            for core, out_ref in ((0, same_ref), (1, other_ref)):
                start = (core * count + i) * PAD
                out_ref[i, :, columns] = rows[start : start + capacity].astype(jnp.bfloat16)


def gate_kernel(capacity, normed_ref, router_ref, ids_ref, out_ref):
    logits = lax.dot_general(
        router_ref[...], normed_ref[...], (((1,), (1,)), ((), ())), preferred_element_type=jnp.float32
    )
    expert = lax.broadcasted_iota(jnp.int32, logits.shape, 0)
    chosen = [
        jnp.sum(jnp.where(expert == ids_ref[k : k + 1, :], logits, 0.0), axis=0, keepdims=True)
        for k in range(2)
    ]
    gate = 1.0 / (1.0 + jnp.exp(chosen[1] - chosen[0]))
    first, second = [
        jnp.where(core == 0, place * TILE, RING * TILE + place * capacity) + rank
        for place, core, rank in slots(ids_ref)
    ]
    row = lax.broadcasted_iota(jnp.int32, out_ref.shape[1:], 0)
    rest = jnp.where(row == first, gate, 0.0) + jnp.where(row == second, 1.0 - gate, 0.0)
    for term in range(3):
        part = rest.astype(jnp.bfloat16)
        out_ref[term] = part
        rest = rest - part.astype(jnp.float32)


def mix_kernel(hidden_ref, weight_ref, own_ref, below_ref, above_ref, across_ref, other_ref, out_ref, held_ref):
    width = hidden_ref.shape[1]
    held_ref[...] = jnp.zeros_like(held_ref)
    for i, ref in enumerate((own_ref, below_ref, above_ref, across_ref, other_ref)):
        held_ref[i * TILE : i * TILE + ref.shape[0], :] = ref[...]
    weights = [weight_ref[term] for term in range(3)]

    @pl.loop(0, width // MIX)
    def _(step):
        columns = pl.ds(pl.multiple_of(step * MIX, MIX), MIX)
        rows = held_ref[:, columns]
        total = 0.0
        for weight in weights[::-1]:
            total = total + lax.dot_general(
                weight, rows, (((0,), (0,)), ((), ())), preferred_element_type=jnp.float32
            )
        out_ref[:, columns] = (hidden_ref[:, columns].astype(jnp.float32) + total).astype(jnp.bfloat16)


def along_x(value, step):
    pairs = [(2 * x + c, 2 * ((x + step) % RING) + c) for x in range(RING) for c in range(2)]
    return lax.ppermute(value, "expert", pairs)


def other_core(value):
    return lax.ppermute(value, "expert", [(i, i ^ 1) for i in range(2 * RING)])


def shift(value, axis, step):
    def target(i):
        z, y = divmod(i, RING)
        return ((z + step) % RING) * RING + y if axis == "z" else z * RING + (y + step) % RING

    return lax.ppermute(value, "hidden", [(i, target(i)) for i in range(RING * RING)])


def gather_ring(own, first, second):
    half = own.shape[1] // 2
    below, above = shift(own, first, 1), shift(own, first, -1)
    across = [shift(below[:, :half], first, 1), shift(above[:, half:], first, -1)]
    mine = jnp.concatenate([own, below, above, jnp.concatenate(across, axis=1)], axis=0)
    mine = lax.optimization_barrier(mine)
    rows = mine.shape[0] // 2
    below, above = shift(mine, second, 1), shift(mine, second, -1)
    far = [shift(below[:rows], second, 1), shift(above[rows:], second, -1)]
    return [mine], [below, above], far


def add(*terms):
    total = terms[0].astype(jnp.float32)
    for term in terms[1:]:
        total = total + term.astype(jnp.float32)
    return total.astype(jnp.bfloat16)


def spread(value, top, left, like):
    rows, columns = like.shape
    pads = (top, rows - top - value.shape[0]), (left, columns - left - value.shape[1])
    return jnp.pad(value, pads)


def reduce_rings(stages, down, orders, rows):
    half = down.shape[1] // 2
    group = RING * rows
    both = range(2)

    def product(blocks):
        value = jnp.concatenate(blocks, axis=0)
        value = jnp.dot(value, down, preferred_element_type=jnp.float32)
        return lax.optimization_barrier(value.astype(jnp.bfloat16))

    def flat(value):
        return value.reshape(-1, value.shape[-1])

    def send(blocks):
        return [
            (shift(block[:, :half], orders[i][0], 1), shift(block[:, half:], orders[i][0], -1))
            for i, block in enumerate(blocks)
        ]

    value = product([flat(stages[0][:, :, 3]), flat(stages[1][:, :, 3])])
    early = send(
        [
            jnp.concatenate(
                [value[i * rows : (i + 1) * rows], value[2 * (i + 1) * rows : 2 * (i + 2) * rows]], axis=0
            )
            for i in both
        ]
    )
    value = product([flat(stages[2][:, :, 3])])
    late = send([value[i * rows : (i + 1) * rows] for i in both])
    outer = [product([flat(act[i, :, 1:3]) for act in stages]).reshape(RING, 2, rows, -1) for i in both]
    kept = product([flat(act[:, :, 0]) for act in stages])
    results = []
    for i in both:
        first, second = orders[i]
        below, above = [outer[i][:, k].reshape(group, -1) for k in range(2)]
        above = add(above, spread(early[i][0], 0, 0, above), spread(late[i][0], 3 * rows, 0, above))
        below = add(below, spread(early[i][1], 0, half, below), spread(late[i][1], 3 * rows, half, below))
        above, below = shift(above, first, 1), shift(below, first, -1)
        own = [
            kept[i * rows : (i + 1) * rows],
            kept[2 * (i + 1) * rows : 2 * (i + 2) * rows],
            kept[(6 + i) * rows : (7 + i) * rows],
        ]
        own = add(jnp.concatenate(own, axis=0), above, below)
        across = own[3 * rows :]
        low = shift(across[:, :half], second, 1)
        high = shift(across[:, half:], second, -1)
        above, below = own[2 * rows : 3 * rows], own[rows : 2 * rows]
        above = shift(add(above, spread(low, 0, 0, above)), second, 1)
        below = shift(add(below, spread(high, 0, half, below)), second, -1)
        results.append(add(own[:rows], above, below))
    return results


def per_device(hidden_in, norm_gain, router_weight, expert_ids, gate_proj, up_proj, down_proj):
    experts = lax.axis_size("expert")
    tok_rows = hidden_in.shape[0]
    width = hidden_in.shape[1]
    top_count = expert_ids.shape[1]
    capacity = 3 * tok_rows * top_count // (2 * experts)
    rows = experts * capacity
    ids = expert_ids.T
    piece = jax.ShapeDtypeStruct((RING, capacity, width), jnp.bfloat16)
    same, other, normed = pl.pallas_call(
        route_kernel,
        out_shape=(piece, piece, jax.ShapeDtypeStruct((tok_rows, width), jnp.bfloat16)),
        name="route",
    )(hidden_in, norm_gain.reshape(1, width), ids)
    weights = pl.pallas_call(
        functools.partial(gate_kernel, capacity),
        out_shape=jax.ShapeDtypeStruct((3, (RING + 2) * TILE, tok_rows), jnp.bfloat16),
        name="gates",
    )(normed, router_weight.T, ids)
    gate_local = gate_proj[0]
    up_local = up_proj[0]
    down_local = down_proj[0]
    other = other_core(other)
    both = [jnp.concatenate([same[i], other[i]], axis=0) for i in range(RING)]
    arrived = [
        jnp.concatenate([both[0], along_x(both[2], 1)], axis=0),
        jnp.concatenate([along_x(both[1], -1), along_x(both[3], 2)], axis=0),
    ]
    arrived = [lax.optimization_barrier(value) for value in arrived]
    part = rows // 2
    orders = (("z", "y"), ("y", "z"))
    gathered = [gather_ring(arrived[i], *orders[i]) for i in range(2)]
    stages = []
    for stage in range(3):
        value = jnp.concatenate(gathered[0][stage] + gathered[1][stage], axis=0)
        gate = jnp.dot(value, gate_local, preferred_element_type=jnp.float32)
        upper = jnp.dot(value, up_local, preferred_element_type=jnp.float32)
        act = (jax.nn.silu(gate) * upper).astype(jnp.bfloat16)
        stages.append(act.reshape(2, -1, RING, part, act.shape[1]))
    answers = reduce_rings(stages, down_local, orders, part)
    half = part // 2
    back = [
        answers[0][:half],
        along_x(answers[1][:half], 1),
        along_x(answers[0][half:], -1),
        along_x(answers[1][half:], 2),
    ]
    crossed = other_core(jnp.concatenate([value[capacity:] for value in back], axis=0))
    return pl.pallas_call(
        mix_kernel,
        out_shape=jax.ShapeDtypeStruct((tok_rows, width), jnp.bfloat16),
        scratch_shapes=[pltpu.VMEM(((RING + 2) * TILE, width), jnp.bfloat16)],
        name="mix",
    )(hidden_in, weights, *back, crossed)


def solution(mesh):
    placed = (
        P(("expert", "hidden"), None),
        P(),
        P(),
        P(("expert", "hidden"), None),
        P("expert", None, "hidden"),
        P("expert", None, "hidden"),
        P("expert", "hidden", None),
    )

    return jax.shard_map(
        per_device,
        mesh=mesh,
        in_specs=placed,
        out_specs=P(("expert", "hidden"), None),
        check_vma=False,
    )
```

time: 194 us -> 179 us (0.923)
  blocking collectives: 17.9 us -> 0 us
  starting transfers between devices: 70.4 us -> 79.7 us
  matrix products: 25.5 us -> 17.3 us
    ppermute x0 -> x8, starting transfers between devices: none -> 28.4 us  [the longest x2 17.9 us: other_core(): return lax.ppermute(value, 'expert', [(i, i ^ 1) for i in range(2 * RING)])]
    all_to_all x1 -> x0, blocking collectives: 17.9 us -> none  [per_device(): lax.all_to_all(outgoing, 'expert', split_axis=0, concat_axis=0, tiled=True)]
    all_to_all x1 -> x0, starting transfers between devices: 17.6 us -> none  [per_device(): lax.all_to_all(answers, 'expert', split_axis=0, concat_axis=0, tiled=True)]
    all_to_all x1 -> x0, waiting for transfers between devices: 10.4 us -> none  [per_device(): lax.all_to_all(answers, 'expert', split_axis=0, concat_axis=0, tiled=True)]
    ppermute x0 -> x8, waiting for transfers between devices: none -> 9.66 us  [the longest x6 9.16 us: along_x(): return lax.ppermute(value, 'expert', pairs)]
    dot_general x14 -> x5, matrix products: 11.8 us -> 6.5 us  [product(): value = jnp.dot(value, down, preferred_element_type=jnp.float32)]
    dot_general x3, matrix products: 8.33 us -> 5.34 us  [per_device(): gate = jnp.dot(value, gate_local, preferred_element_type=jnp.float32)]
    ppermute x36, waiting for transfers between devices: 52.8 us -> 54.8 us  [shift(): lax.ppermute(value, 'hidden', [(i, target(i)) for i in range(RING * RING)])]
  transfers between devices with their start and end apart: 37 -> 44, of which waited for: 12 -> 18; matrix products, arithmetic and copies ran while one was open for 11% -> 9% of each run, Pallas kernels for 1% -> 1%
where the time goes in v2:
time: 179 us
  starting transfers between devices  79.7 us (45%)
  waiting for transfers between devices  64.4 us (36%)
  matrix products  17.3 us (10%)
  Pallas kernels  9.16 us (5%)
  local copies, waits for them, and re-layouts  4.28 us (2%)
  other arithmetic  3.44 us (2%)
    ppermute x36, waiting for transfers between devices, shift(): lax.ppermute(value, 'hidden', [(i, target(i)) for i in range(RING * RING)])  54.8 us
    ppermute x36, starting transfers between devices, shift(): lax.ppermute(value, 'hidden', [(i, target(i)) for i in range(RING * RING)])  51.3 us
    ppermute x2, starting transfers between devices, other_core(): return lax.ppermute(value, 'expert', [(i, i ^ 1) for i in range(2 * RING)])  17.9 us
    ppermute x6, starting transfers between devices, along_x(): return lax.ppermute(value, 'expert', pairs)  10.6 us
    ppermute x6, waiting for transfers between devices, along_x(): return lax.ppermute(value, 'expert', pairs)  9.16 us
    dot_general x5, matrix products, product(): value = jnp.dot(value, down, preferred_element_type=jnp.float32)  6.5 us
    dot_general x3, matrix products, per_device(): upper = jnp.dot(value, up_local, preferred_element_type=jnp.float32)  5.42 us
    dot_general x3, matrix products, per_device(): gate = jnp.dot(value, gate_local, preferred_element_type=jnp.float32)  5.34 us
  transfers between devices with their start and end apart: 44, of which 18 were waited for; matrix products, arithmetic and copies ran while one was open for 9% of the time, Pallas kernels for 1%

profile of v2, /device:TPU:1, one launch (start us, length us, event | category | flops | bytes accessed | tf_op | source)
XLA Modules:
  0.0 179.0 jit_solution(10276757845529951619)
XLA Ops:
  0.0 3.7 %route.1 = (bf16[4,6,6144]{2,1,0:T(8,128)(2,1)}, bf16[4,6,6144]{2,1,0:T(8,128)(2,1)}, bf16[16,6144]{1,0:T(8,128)(2,1)}) custom-call(bf16[16,6144]{1,0:T(8,128)(2,1)} %hidden_ref.3, f32[1,6144]{1,0:T(1,128)} %bitcast.117, s32[2,16]{1,0:T(2,128)} %bitcast.118), custom_call_target="tpu_custom_call" | custom-call | tf_op jit(solution)/shard_map/route/pallas_call | solution.py:208
  8.2 2.5 %collective-permute-start.7 = (bf16[12,6144]{1,0:T(8,128)(2,1)S(1)}, bf16[12,6144]{1,0:T(8,128)(2,1)S(1)}, u32[]{:S(2)}, u32[]{:S(2)}) collective-permute-start(bf16[12,6144]{1,0:T(8,128)(2,1)S(1)} %pad_maximum_fusion.14), channel_id=1, source_target_pairs={{0,64},{16,80},{32,96},{48,112},{64,0},{80,16},{96,32},{112,48},{1... | collective-permute-start | bytes 442376 | tf_op jit(solution)/shard_map/ppermute | solution.py:104
  14.2 3.9 %collective-permute-start.3 = (bf16[24,6144]{1,0:T(8,128)(2,1)S(1)}, bf16[24,6144]{1,0:T(8,128)(2,1)S(1)}, u32[]{:S(2)}, u32[]{:S(2)}) collective-permute-start(bf16[24,6144]{1,0:T(8,128)(2,1)S(1)} %pad_maximum_fusion.9), channel_id=1, source_target_pairs={{0,12},{1,13},{2,14},{3,15},{4,0},{5,1},{6,2},{7,3},{8,4},{9,5},{1... | collective-permute-start | bytes 884744 | tf_op jit(solution)/shard_map/ppermute | solution.py:116
  19.5 2.8 %collective-permute-start.9 = (bf16[24,6144]{1,0:T(8,128)(2,1)S(1)}, bf16[24,6144]{1,0:T(8,128)(2,1)S(1)}, u32[]{:S(2)}, u32[]{:S(2)}) collective-permute-start(bf16[24,6144]{1,0:T(8,128)(2,1)S(1)} %pad_maximum_fusion.10), channel_id=1, source_target_pairs={{0,3},{1,0},{2,1},{3,2},{4,7},{5,4},{6,5},{7,6},{8,11},{9,8},{10,9... | collective-permute-start | bytes 884744 | tf_op jit(solution)/shard_map/ppermute | solution.py:116
  23.3 3.5 %collective-permute-start.5 = (bf16[24,3072]{1,0:T(8,128)(2,1)S(1)}, bf16[24,3072]{1,0:T(8,128)(2,1)S(1)}, u32[]{:S(2)}, u32[]{:S(2)}) collective-permute-start(bf16[24,3072]{1,0:T(8,128)(2,1)S(1)} %slice.288), channel_id=1, source_target_pairs={{0,12},{1,13},{2,14},{3,15},{4,0},{5,1},{6,2},{7,3},{8,4},{9,5},{1... | collective-permute-start | bytes 442376 | tf_op jit(solution)/shard_map/ppermute | solution.py:116
  27.4 3.5 %collective-permute-start.11 = (bf16[24,3072]{1,0:T(8,128)(2,1)S(1)}, bf16[24,3072]{1,0:T(8,128)(2,1)S(1)}, u32[]{:S(2)}, u32[]{:S(2)}) collective-permute-start(bf16[24,3072]{1,0:T(8,128)(2,1)S(1)} %slice.292), channel_id=1, source_target_pairs={{0,3},{1,0},{2,1},{3,2},{4,7},{5,4},{6,5},{7,6},{8,11},{9,8},{10,9... | collective-permute-start | bytes 442376 | tf_op jit(solution)/shard_map/ppermute | solution.py:116
  36.3 3.8 %collective-permute-start.15 = (bf16[96,6144]{1,0:T(8,128)(2,1)S(1)}, bf16[96,6144]{1,0:T(8,128)(2,1)S(1)}, u32[]{:S(2)}, u32[]{:S(2)}) collective-permute-start(bf16[96,6144]{1,0:T(8,128)(2,1)S(1)} %maximum_maximum_fusion.1), channel_id=1, source_target_pairs={{0,12},{1,13},{2,14},{3,15},{4,0},{5,1},{6,2},{7,3},{8,4},{9,5},{1... | collective-permute-start | bytes 3538952 | tf_op jit(solution)/shard_map/ppermute | solution.py:116
  43.0 17.8 %collective-permute-done.12 = bf16[96,6144]{1,0:T(8,128)(2,1)S(1)} collective-permute-done((bf16[96,6144]{1,0:T(8,128)(2,1)S(1)}, bf16[96,6144]{1,0:T(8,128)(2,1)S(1)}, u32[]{:S(2)}, u32[]{:S(2)}) %collective-permute-start.12) | collective-permute-done | bytes 1179680 | tf_op jit(solution)/shard_map/ppermute | solution.py:116
  61.0 2.5 %collective-permute-done.14 = bf16[96,6144]{1,0:T(8,128)(2,1)S(1)} collective-permute-done((bf16[96,6144]{1,0:T(8,128)(2,1)S(1)}, bf16[96,6144]{1,0:T(8,128)(2,1)S(1)}, u32[]{:S(2)}, u32[]{:S(2)}) %collective-permute-start.14) | collective-permute-done | bytes 1179680 | tf_op jit(solution)/shard_map/ppermute | solution.py:116
  63.7 2.6 %fusion.13 = f32[384,512]{1,0:T(8,128)S(1)} fusion(bf16[384,6144]{1,0:T(8,128)(2,1)S(1)} %constant_dynamic-update-slice_fusion, bf16[1,6144,512]{2,1,0:T(8,128)(2,1)S(1)} %copy-done.4), kind=kOutput, calls=%fused_computation.18 | convolution fusion | flops 2415919104 | bytes 11796480 | tf_op jit(solution)/shard_map/dot_general | solution.py:234
  66.3 2.6 %multiply_convert_fusion = bf16[384,512]{1,0:T(8,128)(2,1)S(1)} fusion(f32[384,512]{1,0:T(8,128)S(1)} %fusion.13, bf16[384,6144]{1,0:T(8,128)(2,1)S(1)} %constant_dynamic-update-slice_fusion, bf16[1,6144,512]{2,1,0:T(8,128)(2,1)S(1)} %bitcast.121), kind=kOutput, calls=%fused_computation.45 | convolution fusion | flops 2417098752 | bytes 12189696 | tf_op jit(solution)/shard_map/dot_general | solution.py:235
  72.0 3.3 %collective-permute-start.19 = (bf16[48,6144]{1,0:T(8,128)(2,1)S(1)}, bf16[48,6144]{1,0:T(8,128)(2,1)S(1)}, u32[]{:S(2)}, u32[]{:S(2)}) collective-permute-start(bf16[48,6144]{1,0:T(8,128)(2,1)S(1)} %slice.298), channel_id=1, source_target_pairs={{0,12},{1,13},{2,14},{3,15},{4,0},{5,1},{6,2},{7,3},{8,4},{9,5},{1... | collective-permute-start | bytes 1769480 | tf_op jit(solution)/shard_map/ppermute | solution.py:116
  75.7 6.9 %collective-permute-done.16 = bf16[48,6144]{1,0:T(8,128)(2,1)S(1)} collective-permute-done((bf16[48,6144]{1,0:T(8,128)(2,1)S(1)}, bf16[48,6144]{1,0:T(8,128)(2,1)S(1)}, u32[]{:S(2)}, u32[]{:S(2)}) %collective-permute-start.16) | collective-permute-done | bytes 589856 | tf_op jit(solution)/shard_map/ppermute | solution.py:116
  82.5 3.8 %collective-permute-start.23 = (bf16[72,3072]{1,0:T(8,128)(2,1)S(1)}, bf16[72,3072]{1,0:T(8,128)(2,1)S(1)}, u32[]{:S(2)}, u32[]{:S(2)}) collective-permute-start(bf16[72,3072]{1,0:T(8,128)(2,1)S(1)} %get-tuple-element.36), channel_id=1, source_target_pairs={{0,12},{1,13},{2,14},{3,15},{4,0},{5,1},{6,2},{7,3},{8,4},{9,5},{1... | collective-permute-start | bytes 1327112 | tf_op jit(solution)/shard_map/ppermute | solution.py:116
  100.5 2.7 %collective-permute-start.34 = (bf16[24,3072]{1,0:T(8,128)(2,1)S(1)}, bf16[24,3072]{1,0:T(8,128)(2,1)S(1)}, u32[]{:S(2)}, u32[]{:S(2)}) collective-permute-start(bf16[24,3072]{1,0:T(8,128)(2,1)S(1)} %get-tuple-element.38), channel_id=1, source_target_pairs={{0,3},{1,0},{2,1},{3,2},{4,7},{5,4},{6,5},{7,6},{8,11},{9,8},{10,9... | collective-permute-start | bytes 442376 | tf_op jit(solution)/shard_map/ppermute | solution.py:116
  107.0 2.7 %collective-permute-start.35 = (bf16[96,6144]{1,0:T(8,128)(2,1)S(1)}, bf16[96,6144]{1,0:T(8,128)(2,1)S(1)}, u32[]{:S(2)}, u32[]{:S(2)}) collective-permute-start(bf16[96,6144]{1,0:T(8,128)(2,1)S(1)} %fusion.18), channel_id=1, source_target_pairs={{0,3},{1,0},{2,1},{3,2},{4,7},{5,4},{6,5},{7,6},{8,11},{9,8},{10,9... | collective-permute-start | bytes 3538952 | tf_op jit(solution)/shard_map/ppermute | solution.py:116
  110.1 11.6 %collective-permute-done.25 = bf16[96,6144]{1,0:T(8,128)(2,1)S(1)} collective-permute-done((bf16[96,6144]{1,0:T(8,128)(2,1)S(1)}, bf16[96,6144]{1,0:T(8,128)(2,1)S(1)}, u32[]{:S(2)}, u32[]{:S(2)}) %collective-permute-start.25) | collective-permute-done | bytes 1179680 | tf_op jit(solution)/shard_map/ppermute | solution.py:116
  121.6 6.5 %collective-permute-done.22 = bf16[96,6144]{1,0:T(8,128)(2,1)S(1)} collective-permute-done((bf16[96,6144]{1,0:T(8,128)(2,1)S(1)}, bf16[96,6144]{1,0:T(8,128)(2,1)S(1)}, u32[]{:S(2)}, u32[]{:S(2)}) %collective-permute-start.22) | collective-permute-done | bytes 1179680 | tf_op jit(solution)/shard_map/ppermute | solution.py:116
  129.7 2.7 %collective-permute-start.28 = (bf16[24,3072]{1,0:T(8,128)(2,1)S(1)}, bf16[24,3072]{1,0:T(8,128)(2,1)S(1)}, u32[]{:S(2)}, u32[]{:S(2)}) collective-permute-start(bf16[24,3072]{1,0:T(8,128)(2,1)S(1)} %get-tuple-element.32), channel_id=1, source_target_pairs={{0,3},{1,0},{2,1},{3,2},{4,7},{5,4},{6,5},{7,6},{8,11},{9,8},{10,9... | collective-permute-start | bytes 442376 | tf_op jit(solution)/shard_map/ppermute | solution.py:116
  137.1 2.7 %collective-permute-start.29 = (bf16[24,6144]{1,0:T(8,128)(2,1)S(1)}, bf16[24,6144]{1,0:T(8,128)(2,1)S(1)}, u32[]{:S(2)}, u32[]{:S(2)}) collective-permute-start(bf16[24,6144]{1,0:T(8,128)(2,1)S(1)} %get-tuple-element.30), channel_id=1, source_target_pairs={{0,3},{1,0},{2,1},{3,2},{4,7},{5,4},{6,5},{7,6},{8,11},{9,8},{10,9... | collective-permute-start | bytes 884744 | tf_op jit(solution)/shard_map/ppermute | solution.py:116
  144.6 2.9 %collective-permute-start.41 = (bf16[12,6144]{1,0:T(8,128)(2,1)S(1)}, bf16[12,6144]{1,0:T(8,128)(2,1)S(1)}, u32[]{:S(2)}, u32[]{:S(2)}) collective-permute-start(bf16[12,6144]{1,0:T(8,128)(2,1)S(1)} %get-tuple-element.55), channel_id=1, source_target_pairs={{0,96},{16,112},{32,0},{48,16},{64,32},{80,48},{96,64},{112,80},{1... | collective-permute-start | bytes 442376 | tf_op jit(solution)/shard_map/ppermute | solution.py:104
  150.3 3.6 %collective-permute-done.42.across_ref = bf16[12,6144]{1,0:T(8,128)(2,1)S(1)} collective-permute-done((bf16[12,6144]{1,0:T(8,128)(2,1)S(1)}, bf16[12,6144]{1,0:T(8,128)(2,1)S(1)}, u32[]{:S(2)}, u32[]{:S(2)}) %collective-permute-start.42) | collective-permute-done | bytes 147488 | tf_op jit(solution)/shard_map/ppermute | solution.py:104
  156.3 16.5 %collective-permute-start.43 = (bf16[24,6144]{1,0:T(8,128)(2,1)S(1)}, bf16[24,6144]{1,0:T(8,128)(2,1)S(1)}, u32[]{:S(2)}, u32[]{:S(2)}) collective-permute-start(bf16[24,6144]{1,0:T(8,128)(2,1)S(1)} %pad_maximum_fusion.11), channel_id=1, source_target_pairs={{0,16},{16,0},{32,48},{48,32},{64,80},{80,64},{96,112},{112,96},{1... | collective-permute-start | bytes 884744 | tf_op jit(solution)/shard_map/ppermute | solution.py:108
  175.4 3.6 %mix.1 = bf16[16,6144]{1,0:T(8,128)(2,1)} custom-call(bf16[16,6144]{1,0:T(8,128)(2,1)} %hidden_ref.3, bf16[3,96,16]{2,1,0:T(8,128)(2,1)} %gates.1.weight_ref, bf16[12,6144]{1,0:T(8,128)(2,1)} %get-tuple-element.56.own_ref, bf16[12,6144]{1,0:T(8,128)(2,1)} %copy-done.2, bf16[12,6144]{1,0:T(8,128)(2,1)} %copy-done, bf16[12,6144]{1,0:T(8,128)(2,1)} %copy-done.1, ...), custom_call_target="tpu_custom_call" | custom-call | tf_op jit(solution)/shard_map/mix/pallas_call | solution.py:247
  (156 shorter events, 59.7 us)
Async XLA Ops:
  8.2 11.2 %collective-permute-start.7 = (bf16[12,6144]{1,0:T(8,128)(2,1)S(1)}, bf16[12,6144]{1,0:T(8,128)(2,1)S(1)}, u32[]{:S(2)}, u32[]{:S(2)}) collective-permute-start(bf16[12,6144]{1,0:T(8,128)(2,1)S(1)} %pad_maximum_fusion.14), channel_id=1, source_target_pairs={{0,64},{16,80},{32,96},{48,112},{64,0},{80,16},{96,32},{112,48},{1... | collective-permute-start | bytes 442376 | tf_op jit(solution)/shard_map/ppermute | solution.py:104
  10.8 8.6 %collective-permute-start.6 = (bf16[12,6144]{1,0:T(8,128)(2,1)S(1)}, bf16[12,6144]{1,0:T(8,128)(2,1)S(1)}, u32[]{:S(2)}, u32[]{:S(2)}) collective-permute-start(bf16[12,6144]{1,0:T(8,128)(2,1)S(1)} %pad_maximum_fusion.13), channel_id=1, source_target_pairs={{0,96},{16,112},{32,0},{48,16},{64,32},{80,48},{96,64},{112,80},{1... | collective-permute-start | bytes 442376 | tf_op jit(solution)/shard_map/ppermute | solution.py:104
  14.2 9.1 %collective-permute-start.3 = (bf16[24,6144]{1,0:T(8,128)(2,1)S(1)}, bf16[24,6144]{1,0:T(8,128)(2,1)S(1)}, u32[]{:S(2)}, u32[]{:S(2)}) collective-permute-start(bf16[24,6144]{1,0:T(8,128)(2,1)S(1)} %pad_maximum_fusion.9), channel_id=1, source_target_pairs={{0,12},{1,13},{2,14},{3,15},{4,0},{5,1},{6,2},{7,3},{8,4},{9,5},{1... | collective-permute-start | bytes 884744 | tf_op jit(solution)/shard_map/ppermute | solution.py:116
  18.2 8.6 %collective-permute-start.2 = (bf16[24,6144]{1,0:T(8,128)(2,1)S(1)}, bf16[24,6144]{1,0:T(8,128)(2,1)S(1)}, u32[]{:S(2)}, u32[]{:S(2)}) collective-permute-start(bf16[24,6144]{1,0:T(8,128)(2,1)S(1)} %pad_maximum_fusion.9), channel_id=1, source_target_pairs={{0,4},{1,5},{2,6},{3,7},{4,8},{5,9},{6,10},{7,11},{8,12},{9,13},{1... | collective-permute-start | bytes 884744 | tf_op jit(solution)/shard_map/ppermute | solution.py:116
  19.5 7.9 %collective-permute-start.9 = (bf16[24,6144]{1,0:T(8,128)(2,1)S(1)}, bf16[24,6144]{1,0:T(8,128)(2,1)S(1)}, u32[]{:S(2)}, u32[]{:S(2)}) collective-permute-start(bf16[24,6144]{1,0:T(8,128)(2,1)S(1)} %pad_maximum_fusion.10), channel_id=1, source_target_pairs={{0,3},{1,0},{2,1},{3,2},{4,7},{5,4},{6,5},{7,6},{8,11},{9,8},{10,9... | collective-permute-start | bytes 884744 | tf_op jit(solution)/shard_map/ppermute | solution.py:116
  22.3 8.6 %collective-permute-start.8 = (bf16[24,6144]{1,0:T(8,128)(2,1)S(1)}, bf16[24,6144]{1,0:T(8,128)(2,1)S(1)}, u32[]{:S(2)}, u32[]{:S(2)}) collective-permute-start(bf16[24,6144]{1,0:T(8,128)(2,1)S(1)} %pad_maximum_fusion.10), channel_id=1, source_target_pairs={{0,1},{1,2},{2,3},{3,0},{4,5},{5,6},{6,7},{7,4},{8,9},{9,10},{10,1... | collective-permute-start | bytes 884744 | tf_op jit(solution)/shard_map/ppermute | solution.py:116
  32.5 28.4 %collective-permute-start.13 = (bf16[96,6144]{1,0:T(8,128)(2,1)S(1)}, bf16[96,6144]{1,0:T(8,128)(2,1)S(1)}, u32[]{:S(2)}, u32[]{:S(2)}) collective-permute-start(bf16[96,6144]{1,0:T(8,128)(2,1)S(1)} %maximum_maximum_fusion), channel_id=1, source_target_pairs={{0,3},{1,0},{2,1},{3,2},{4,7},{5,4},{6,5},{7,6},{8,11},{9,8},{10,9... | collective-permute-start | bytes 3538952 | tf_op jit(solution)/shard_map/ppermute | solution.py:116
  35.0 25.8 %collective-permute-start.12 = (bf16[96,6144]{1,0:T(8,128)(2,1)S(1)}, bf16[96,6144]{1,0:T(8,128)(2,1)S(1)}, u32[]{:S(2)}, u32[]{:S(2)}) collective-permute-start(bf16[96,6144]{1,0:T(8,128)(2,1)S(1)} %maximum_maximum_fusion), channel_id=1, source_target_pairs={{0,1},{1,2},{2,3},{3,0},{4,5},{5,6},{6,7},{7,4},{8,9},{9,10},{10,1... | collective-permute-start | bytes 3538952 | tf_op jit(solution)/shard_map/ppermute | solution.py:116
  36.3 27.3 %collective-permute-start.15 = (bf16[96,6144]{1,0:T(8,128)(2,1)S(1)}, bf16[96,6144]{1,0:T(8,128)(2,1)S(1)}, u32[]{:S(2)}, u32[]{:S(2)}) collective-permute-start(bf16[96,6144]{1,0:T(8,128)(2,1)S(1)} %maximum_maximum_fusion.1), channel_id=1, source_target_pairs={{0,12},{1,13},{2,14},{3,15},{4,0},{5,1},{6,2},{7,3},{8,4},{9,5},{1... | collective-permute-start | bytes 3538952 | tf_op jit(solution)/shard_map/ppermute | solution.py:116
  40.1 23.4 %collective-permute-start.14 = (bf16[96,6144]{1,0:T(8,128)(2,1)S(1)}, bf16[96,6144]{1,0:T(8,128)(2,1)S(1)}, u32[]{:S(2)}, u32[]{:S(2)}) collective-permute-start(bf16[96,6144]{1,0:T(8,128)(2,1)S(1)} %maximum_maximum_fusion.1), channel_id=1, source_target_pairs={{0,4},{1,5},{2,6},{3,7},{4,8},{5,9},{6,10},{7,11},{8,12},{9,13},{1... | collective-permute-start | bytes 3538952 | tf_op jit(solution)/shard_map/ppermute | solution.py:116
  70.3 16.1 %collective-permute-start.17 = (bf16[48,6144]{1,0:T(8,128)(2,1)S(1)}, bf16[48,6144]{1,0:T(8,128)(2,1)S(1)}, u32[]{:S(2)}, u32[]{:S(2)}) collective-permute-start(bf16[48,6144]{1,0:T(8,128)(2,1)S(1)} %slice.296), channel_id=1, source_target_pairs={{0,3},{1,0},{2,1},{3,2},{4,7},{5,4},{6,5},{7,6},{8,11},{9,8},{10,9... | collective-permute-start | bytes 1769480 | tf_op jit(solution)/shard_map/ppermute | solution.py:116
  71.8 10.7 %collective-permute-start.16 = (bf16[48,6144]{1,0:T(8,128)(2,1)S(1)}, bf16[48,6144]{1,0:T(8,128)(2,1)S(1)}, u32[]{:S(2)}, u32[]{:S(2)}) collective-permute-start(bf16[48,6144]{1,0:T(8,128)(2,1)S(1)} %slice.295), channel_id=1, source_target_pairs={{0,1},{1,2},{2,3},{3,0},{4,5},{5,6},{6,7},{7,4},{8,9},{9,10},{10,1... | collective-permute-start | bytes 1769480 | tf_op jit(solution)/shard_map/ppermute | solution.py:116
  72.0 17.5 %collective-permute-start.19 = (bf16[48,6144]{1,0:T(8,128)(2,1)S(1)}, bf16[48,6144]{1,0:T(8,128)(2,1)S(1)}, u32[]{:S(2)}, u32[]{:S(2)}) collective-permute-start(bf16[48,6144]{1,0:T(8,128)(2,1)S(1)} %slice.298), channel_id=1, source_target_pairs={{0,12},{1,13},{2,14},{3,15},{4,0},{5,1},{6,2},{7,3},{8,4},{9,5},{1... | collective-permute-start | bytes 1769480 | tf_op jit(solution)/shard_map/ppermute | solution.py:116
  75.3 12.4 %collective-permute-start.18 = (bf16[48,6144]{1,0:T(8,128)(2,1)S(1)}, bf16[48,6144]{1,0:T(8,128)(2,1)S(1)}, u32[]{:S(2)}, u32[]{:S(2)}) collective-permute-start(bf16[48,6144]{1,0:T(8,128)(2,1)S(1)} %slice.297), channel_id=1, source_target_pairs={{0,4},{1,5},{2,6},{3,7},{4,8},{5,9},{6,10},{7,11},{8,12},{9,13},{1... | collective-permute-start | bytes 1769480 | tf_op jit(solution)/shard_map/ppermute | solution.py:116
  75.5 25.0 %collective-permute-start.20 = (bf16[72,3072]{1,0:T(8,128)(2,1)S(1)}, bf16[72,3072]{1,0:T(8,128)(2,1)S(1)}, u32[]{:S(2)}, u32[]{:S(2)}) collective-permute-start(bf16[72,3072]{1,0:T(8,128)(2,1)S(1)} %get-tuple-element.35), channel_id=1, source_target_pairs={{0,4},{1,5},{2,6},{3,7},{4,8},{5,9},{6,10},{7,11},{8,12},{9,13},{1... | collective-permute-start | bytes 1327112 | tf_op jit(solution)/shard_map/ppermute | solution.py:116
  82.5 17.0 %collective-permute-start.23 = (bf16[72,3072]{1,0:T(8,128)(2,1)S(1)}, bf16[72,3072]{1,0:T(8,128)(2,1)S(1)}, u32[]{:S(2)}, u32[]{:S(2)}) collective-permute-start(bf16[72,3072]{1,0:T(8,128)(2,1)S(1)} %get-tuple-element.36), channel_id=1, source_target_pairs={{0,12},{1,13},{2,14},{3,15},{4,0},{5,1},{6,2},{7,3},{8,4},{9,5},{1... | collective-permute-start | bytes 1327112 | tf_op jit(solution)/shard_map/ppermute | solution.py:116
  86.4 23.2 %collective-permute-start.30 = (bf16[72,3072]{1,0:T(8,128)(2,1)S(1)}, bf16[72,3072]{1,0:T(8,128)(2,1)S(1)}, u32[]{:S(2)}, u32[]{:S(2)}) collective-permute-start(bf16[72,3072]{1,0:T(8,128)(2,1)S(1)} %get-tuple-element.33), channel_id=1, source_target_pairs={{0,1},{1,2},{2,3},{3,0},{4,5},{5,6},{6,7},{7,4},{8,9},{9,10},{10,1... | collective-permute-start | bytes 1327112 | tf_op jit(solution)/shard_map/ppermute | solution.py:116
  87.8 18.3 %collective-permute-start.33 = (bf16[72,3072]{1,0:T(8,128)(2,1)S(1)}, bf16[72,3072]{1,0:T(8,128)(2,1)S(1)}, u32[]{:S(2)}, u32[]{:S(2)}) collective-permute-start(bf16[72,3072]{1,0:T(8,128)(2,1)S(1)} %get-tuple-element.34), channel_id=1, source_target_pairs={{0,3},{1,0},{2,1},{3,2},{4,7},{5,4},{6,5},{7,6},{8,11},{9,8},{10,9... | collective-permute-start | bytes 1327112 | tf_op jit(solution)/shard_map/ppermute | solution.py:116
  99.5 10.1 %collective-permute-start.31 = (bf16[24,3072]{1,0:T(8,128)(2,1)S(1)}, bf16[24,3072]{1,0:T(8,128)(2,1)S(1)}, u32[]{:S(2)}, u32[]{:S(2)}) collective-permute-start(bf16[24,3072]{1,0:T(8,128)(2,1)S(1)} %get-tuple-element.37), channel_id=1, source_target_pairs={{0,1},{1,2},{2,3},{3,0},{4,5},{5,6},{6,7},{7,4},{8,9},{9,10},{10,1... | collective-permute-start | bytes 442376 | tf_op jit(solution)/shard_map/ppermute | solution.py:116
  104.9 16.7 %collective-permute-start.25 = (bf16[96,6144]{1,0:T(8,128)(2,1)S(1)}, bf16[96,6144]{1,0:T(8,128)(2,1)S(1)}, u32[]{:S(2)}, u32[]{:S(2)}) collective-permute-start(bf16[96,6144]{1,0:T(8,128)(2,1)S(1)} %fusion.22), channel_id=1, source_target_pairs={{0,12},{1,13},{2,14},{3,15},{4,0},{5,1},{6,2},{7,3},{8,4},{9,5},{1... | collective-permute-start | bytes 3538952 | tf_op jit(solution)/shard_map/ppermute | solution.py:116
  106.1 22.1 %collective-permute-start.22 = (bf16[96,6144]{1,0:T(8,128)(2,1)S(1)}, bf16[96,6144]{1,0:T(8,128)(2,1)S(1)}, u32[]{:S(2)}, u32[]{:S(2)}) collective-permute-start(bf16[96,6144]{1,0:T(8,128)(2,1)S(1)} %fusion.24), channel_id=1, source_target_pairs={{0,4},{1,5},{2,6},{3,7},{4,8},{5,9},{6,10},{7,11},{8,12},{9,13},{1... | collective-permute-start | bytes 3538952 | tf_op jit(solution)/shard_map/ppermute | solution.py:116
  107.0 21.2 %collective-permute-start.35 = (bf16[96,6144]{1,0:T(8,128)(2,1)S(1)}, bf16[96,6144]{1,0:T(8,128)(2,1)S(1)}, u32[]{:S(2)}, u32[]{:S(2)}) collective-permute-start(bf16[96,6144]{1,0:T(8,128)(2,1)S(1)} %fusion.18), channel_id=1, source_target_pairs={{0,3},{1,0},{2,1},{3,2},{4,7},{5,4},{6,5},{7,6},{8,11},{9,8},{10,9... | collective-permute-start | bytes 3538952 | tf_op jit(solution)/shard_map/ppermute | solution.py:116
  109.9 18.3 %collective-permute-start.32 = (bf16[96,6144]{1,0:T(8,128)(2,1)S(1)}, bf16[96,6144]{1,0:T(8,128)(2,1)S(1)}, u32[]{:S(2)}, u32[]{:S(2)}) collective-permute-start(bf16[96,6144]{1,0:T(8,128)(2,1)S(1)} %fusion.20), channel_id=1, source_target_pairs={{0,1},{1,2},{2,3},{3,0},{4,5},{5,6},{6,7},{7,4},{8,9},{9,10},{10,1... | collective-permute-start | bytes 3538952 | tf_op jit(solution)/shard_map/ppermute | solution.py:116
  156.3 18.3 %collective-permute-start.43 = (bf16[24,6144]{1,0:T(8,128)(2,1)S(1)}, bf16[24,6144]{1,0:T(8,128)(2,1)S(1)}, u32[]{:S(2)}, u32[]{:S(2)}) collective-permute-start(bf16[24,6144]{1,0:T(8,128)(2,1)S(1)} %pad_maximum_fusion.11), channel_id=1, source_target_pairs={{0,16},{16,0},{32,48},{48,32},{64,80},{80,64},{96,112},{112,96},{1... | collective-permute-start | bytes 884744 | tf_op jit(solution)/shard_map/ppermute | solution.py:108
  (29 other events, 235.4 us)
